TPU v7x, 128 devices: a whole 4x4x4 slice. The times are simulated.
128 devices in a mesh: seq: 16 (over x, z), nbr: 4 (over y), batch: 2 (over core).
Axes of the slice: x: 4, y: 4, z: 4, core: 2. Of those that a mesh axis runs over, the one named last changes fastest.
Arguments:
- hidden: bfloat16 [4096, 4096], P(('batch', 'seq'), 'nbr'), parts along dimension 0, may hold values from -6 to 6
- d_out: bfloat16 [4096, 4096], P(('batch', 'seq'), 'nbr'), parts along dimension 0, may hold values from -6 to 6
- nbr_emb: bfloat16 [768, 128, 896], P(('batch', 'seq', 'nbr')), parts along dimension 0, may hold values from -6 to 6
- slot_span: int32 [768], P(('batch', 'seq')), parts along dimension 0, may hold values from -1 to 1, as said below
- dec_gain: bfloat16 [4096], P('nbr'), may hold values from 0.5 to 1.5
- enc_gain: bfloat16 [896], replicated, may hold values from 0.5 to 1.5
- w_cond: bfloat16 [4096, 896], P('nbr'), may hold values from -0.75 to 0.75
- w_enc: bfloat16 [896, 896], replicated, may hold values from -0.1875 to 0.1875
- w_q: bfloat16 [4096, 2048], P('seq', 'nbr'), may hold values from -0.09375 to 0.09375
- w_k: bfloat16 [896, 2048], P('seq', 'nbr'), may hold values from -8 to 8
- w_v: bfloat16 [896, 2048], P('seq', 'nbr'), may hold values from -0.1875 to 0.1875
- w_o: bfloat16 [2048, 4096], P('nbr', 'seq'), may hold values from -0.125 to 0.125
Outputs:
- out: bfloat16 [4096, 4096], P(('batch', 'seq'), 'nbr'), parts along dimension 0
- d_hidden: bfloat16 [4096, 4096], P(('batch', 'seq'), 'nbr'), parts along dimension 0
- d_enc: bfloat16 [768, 128, 896], P(('batch', 'seq', 'nbr')), parts along dimension 0
- d_wo: float32 [4096, 4096], P(('batch', 'nbr'), 'seq'), parts along dimension 0
- d_wk: float32 [1792, 2048], P(('batch', 'seq'), 'nbr'), parts along dimension 0
- d_wv: float32 [1792, 2048], P(('batch', 'seq'), 'nbr'), parts along dimension 0
There are 2 independent parts, one for each index of `batch`. A program takes and returns all parts, laid end to end along the dimension named above; an argument that names none is the same for every part. Nothing has to cross between parts.
Inputs may be any that keep to these rules, and one draw needn't show every extreme that they name: `slot_span`: A slot on seq index s serves a span of seq index s, counted from 0 within its 2 spans; -1 marks an empty slot. Every span is served by 1 to 8 slots, and one span of each seq index by exactly 8. Within each seq index one nbr index has all 6 slots live.
All inputs are finite; a program needn't handle non-finite values.
Results may differ from a plain program's by a relative error of at most 0.018.
The roundings to bfloat16 on the way count: a program that leaves them out, or rounds other values in their place, can miss the bound.
Values may be sent and summed in bfloat16 or wider, within the bound.
No kernel may reach another device: no remote copies, remote signals or barrier semaphores. Data moves between devices by JAX's collectives and lax.ppermute only.
A program may use at most 128 MiB of HBM per device.

v0:
```python
import jax
import jax.numpy as jnp
from jax import lax
from jax.sharding import PartitionSpec as P

HD = 128
CLEN = 64
NLEN = 128


def rows_first(arrays, axis, dims):
    turned = [jnp.moveaxis(a, dim, 0) for a, dim in zip(arrays, dims)]
    both = jnp.concatenate([t.reshape(len(t), -1) for t in turned], axis=1)
    whole, at, done = (lax.all_gather(both, axis, axis=0, tiled=True), 0, [])
    for t, dim in zip(turned, dims):
        share = whole[:, at : at + t[0].size].reshape(-1, *t.shape[1:])
        done.append(jnp.moveaxis(share, 0, dim))
        at += t[0].size
    return tuple(done)


def shifted(shard, axis, by):
    length = lax.axis_size(axis)
    pairs = [(i, i + by) for i in range(length) if 0 <= i + by < length]
    return lax.ppermute(shard, axis, pairs)


def sent_to_all(shard, axis):
    copies = jnp.broadcast_to(shard, (lax.axis_size(axis), *shard.shape))
    return lax.all_to_all(copies, axis, split_axis=0, concat_axis=0, tiled=True)


def over_copies(shard, axis):
    return sent_to_all(shard, axis).sum(axis=0)


def in_order(parts, dim):
    dims = list(parts.shape[1:])
    dims[dim] *= parts.shape[0]
    return jnp.moveaxis(parts, 0, dim).reshape(dims)


def one_gather(arrays, axis, dims):
    vector = jnp.concatenate([a.reshape(-1) for a in arrays])
    lines, at, done = (lax.all_gather(vector, axis), 0, [])
    for a, dim in zip(arrays, dims):
        parts = lines[:, at : at + a.size].reshape(-1, *a.shape)
        done.append(in_order(parts, dim))
        at += a.size
    return tuple(done)


def collect(shard, axis, dim):
    parts = sent_to_all(shard, axis)
    return in_order(parts, dim)


def in_blocks(shard, dim, length):
    dims = shard.shape
    parts = shard.reshape(*dims[:dim], length, dims[dim] // length, *dims[dim + 1 :])
    return jnp.moveaxis(parts, dim, 0)


def sent_and_summed(shard, axis, dim):
    parts = in_blocks(shard, dim, lax.axis_size(axis))
    arrived = lax.all_to_all(parts, axis, split_axis=0, concat_axis=0, tiled=True)
    return arrived.astype(jnp.float32).sum(axis=0)


def in_one_piece(arrays, axis, dim, along):
    ends, at = ([], 0)
    for a in arrays[:-1]:
        at += a.shape[along]
        ends.append(at)
    both = jnp.concatenate(arrays, axis=along)
    return tuple(
        jnp.split(lax.psum_scatter(both, axis, scatter_dimension=dim, tiled=True), ends, axis=along)
    )


def rms_scale(values):
    return lax.rsqrt(jnp.mean(values * values, axis=-1, keepdims=True) + 1e-06)


def body(hidden, d_out, nbr_emb, slot_span, dec_gain, enc_gain, w_cond, w_enc, w_q, w_k, w_v, w_o):
    single = jnp.float32
    brain = jnp.bfloat16
    factor = HD ** (-0.5)
    hid_all, dout_all, gain_all = rows_first((hidden, d_out, dec_gain), "nbr", (1, 1, 0))
    tokens = hidden.shape[0]
    spans = tokens // CLEN
    pooled = jnp.mean(hidden.astype(single).reshape(spans, CLEN, hidden.shape[1]), axis=1).astype(
        brain
    )
    carried = shifted(pooled[spans - 1 :], "seq", 1)
    before = jnp.concatenate([carried, pooled[: spans - 1]], axis=0)
    condition = over_copies(jnp.dot(before, w_cond, preferred_element_type=single), "nbr")
    slots = nbr_emb.shape[0]
    own_span = lax.dynamic_slice_in_dim(slot_span, lax.axis_index("nbr") * slots, slots)
    lookup = (own_span[:, None] == jnp.arange(spans, dtype=jnp.int32)[None, :]).astype(single)
    slot_cond = jnp.dot(lookup, condition, precision=lax.Precision.HIGHEST)
    inputs = nbr_emb.astype(single) + slot_cond[:, None, :]
    width = inputs.shape[2]
    enc_normed = (inputs * rms_scale(inputs) * enc_gain.astype(single)).astype(brain)
    mixed = jnp.dot(enc_normed.reshape(-1, width), w_enc, preferred_element_type=single).reshape(
        inputs.shape
    )
    encoded = (inputs + jax.nn.silu(mixed)).astype(brain)
    wq_all, wk_all, wv_all, wo_all = one_gather((w_q, w_k, w_v, w_o), "seq", (0, 0, 0, 1))
    group_enc = collect(encoded, "nbr", 0)
    enc_rows = group_enc.reshape(-1, width)
    hf = hid_all.astype(single)
    rstd = rms_scale(hf)
    normed = (hf * rstd * gain_all.astype(single)).astype(brain)
    query = jnp.dot(normed, wq_all, preferred_element_type=single).astype(brain)
    keys = jnp.dot(enc_rows, wk_all, preferred_element_type=single).astype(brain)
    values = jnp.dot(enc_rows, wv_all, preferred_element_type=single).astype(brain)
    local_width = query.shape[1]
    heads = local_width // HD
    query3 = query.reshape(tokens, heads, HD)
    keys3 = keys.reshape(-1, heads, HD)
    values3 = values.reshape(-1, heads, HD)
    token_span = jnp.arange(tokens, dtype=jnp.int32) // CLEN
    key_span = jnp.repeat(slot_span, NLEN)
    allowed = token_span[:, None] == key_span[None, :]
    scores = jnp.einsum("thd,khd->htk", query3, keys3, preferred_element_type=single) * factor
    scores = jnp.where(allowed[None], scores, -1e30)
    peak = jnp.max(scores, axis=-1, keepdims=True)
    weights = jnp.exp(scores - peak)
    probs = weights / jnp.sum(weights, axis=-1, keepdims=True)
    probs_b = probs.astype(brain)
    attended = jnp.einsum("htk,khd->thd", probs_b, values3, preferred_element_type=single)
    attended = attended.reshape(tokens, local_width).astype(brain)
    partial_out = jnp.dot(attended, wo_all, preferred_element_type=single)
    summed = sent_and_summed(partial_out.astype(jnp.bfloat16), "nbr", 1)
    out = (hidden.astype(single) + summed).astype(brain)
    d_attn = jnp.dot(dout_all, wo_all.T, preferred_element_type=single).astype(brain)
    d_attn3 = d_attn.reshape(tokens, heads, HD)
    d_probs = jnp.einsum("thd,khd->htk", d_attn3, values3, preferred_element_type=single)
    row_dot = jnp.sum(probs * d_probs, axis=-1, keepdims=True)
    d_scores = (probs * (d_probs - row_dot) * factor).astype(brain)
    d_query = jnp.einsum("htk,khd->thd", d_scores, keys3, preferred_element_type=single)
    d_query = d_query.reshape(tokens, local_width).astype(brain)
    d_key = jnp.einsum("htk,thd->khd", d_scores, query3, preferred_element_type=single)
    d_key = d_key.reshape(-1, local_width).astype(brain)
    d_value = jnp.einsum("htk,thd->khd", probs_b, d_attn3, preferred_element_type=single)
    d_value = d_value.reshape(-1, local_width).astype(brain)
    wo_partial = jnp.dot(attended.T, dout_all, preferred_element_type=single)
    d_wo = lax.psum_scatter(
        wo_partial.astype(jnp.bfloat16), "seq", scatter_dimension=1, tiled=True
    ).astype(jnp.float32)
    d_wk, d_wv = tuple(
        (
            part.astype(jnp.float32)
            for part in in_one_piece(
                (
                    jnp.dot(enc_rows.T, d_key, preferred_element_type=single).astype(jnp.bfloat16),
                    jnp.dot(enc_rows.T, d_value, preferred_element_type=single).astype(
                        jnp.bfloat16
                    ),
                ),
                "seq",
                0,
                1,
            )
        )
    )
    enc_term = jnp.dot(d_key, wk_all.T, preferred_element_type=single) + jnp.dot(
        d_value, wv_all.T, preferred_element_type=single
    )
    d_enc = sent_and_summed(
        enc_term.reshape(group_enc.shape).astype(jnp.bfloat16), "nbr", 0
    ).astype(brain)
    d_normed = jnp.dot(d_query, wq_all.T, preferred_element_type=single)
    full_width = hf.shape[1]
    own_grad = sent_and_summed(d_normed.astype(jnp.bfloat16), "nbr", 1)
    own_states = hidden.astype(single)
    scaled_grad = dec_gain.astype(single) * own_grad
    partial_stat = jnp.sum(own_states * scaled_grad, axis=-1, keepdims=True) / full_width
    stat = over_copies(partial_stat, "nbr")
    d_hidden = d_out.astype(single) + rstd * scaled_grad - own_states * rstd**3 * stat
    return (out, d_hidden.astype(brain), d_enc, d_wo, d_wk, d_wv)


def solution(mesh):
    placed = (
        P(("batch", "seq"), "nbr"),
        P(("batch", "seq"), "nbr"),
        P(("batch", "seq", "nbr"), None, None),
        P(("batch", "seq")),
        P("nbr"),
        P(),
        P("nbr", None),
        P(),
        P("seq", "nbr"),
        P("seq", "nbr"),
        P("seq", "nbr"),
        P("nbr", "seq"),
    )
    return jax.shard_map(
        body,
        mesh=mesh,
        in_specs=placed,
        out_specs=(
            P(("batch", "seq"), "nbr"),
            P(("batch", "seq"), "nbr"),
            P(("batch", "seq", "nbr"), None, None),
            P(("batch", "nbr"), "seq"),
            P(("batch", "seq"), "nbr"),
            P(("batch", "seq"), "nbr"),
        ),
        check_vma=False,
    )
```

profile of v0, /device:TPU:0, one launch (start us, length us, event | category | flops | bytes accessed | tf_op | source)
XLA Modules:
  0.0 406.9 jit_solution(13471765406309649294)
XLA Ops:
  8.1 1.9 pad_maximum_fusion.2
  15.0 3.9 collective-permute-start
  19.0 1.2 collective-permute-done
  21.2 4.5 %all-to-all-start = ((f32[4,2,896]{2,1,0:T(2,128)}), f32[4,2,896]{2,1,0:T(2,128)S(1)}, u32[]{:S(2)}, u32[]{:S(2)}) async-start(f32[4,2,896]{2,1,0:T(2,128)} %broadcast_in_dim.20), calls=%async_computation | async-start | bytes 57344 | tf_op jit(solution)/shard_map/all_to_all | solution.py:30
  26.0 5.3 %all-to-all-done = f32[4,2,896]{2,1,0:T(2,128)S(1)} async-done(((f32[4,2,896]{2,1,0:T(2,128)}), f32[4,2,896]{2,1,0:T(2,128)S(1)}, u32[]{:S(2)}, u32[]{:S(2)}) %all-to-all-start) | async-done | bytes 28704 | tf_op jit(solution)/shard_map/all_to_all | solution.py:30
  31.6 1.8 multiply_reduce_fusion.1
  33.4 4.3 %add_convert_fusion.1 = bf16[6,128,896]{2,1,0:T(8,128)(2,1)S(1)} fusion(bf16[6,128,896]{2,1,0:T(8,128)(2,1)} %param.14, bf16[896,896]{1,0:T(8,128)(2,1)} %param.19, f32[896]{0:T(1024)S(1)} %convert_element_type.151, f32[6,128]{1,0:T(8,128)S(1)} %add_rsqrt_fusion, f32[6,896]{1,0:T(8,128)S(1)} %fusion.45), kind=kOutput, calls=%fused_computation.21 | convolution fusion | flops 1242071040 | bytes 4386304 | tf_op jit(solution)/shard_map/dot_general | solution.py:105
  37.7 3.3 broadcast_in_dim.21
  40.9 5.1 %all-to-all-start.1 = ((bf16[4,6,128,896]{3,2,1,0:T(8,128)(2,1)}), bf16[4,6,128,896]{3,2,1,0:T(8,128)(2,1)}, u32[]{:S(2)}, u32[]{:S(2)}) async-start(bf16[4,6,128,896]{3,2,1,0:T(8,128)(2,1)} %broadcast_in_dim.21), calls=%async_computation.1 | async-start | bytes 11010048 | tf_op jit(solution)/shard_map/all_to_all | solution.py:30
  46.7 1.5 fusion.14
  49.6 76.9 %all-gather.6.cloned.1.call-done = bf16[5111808]{0:T(1024)(128)(2,1)} async-done(((bf16[319488]{0:T(1024)(128)(2,1)}), bf16[5111808]{0:T(1024)(128)(2,1)}) %all-gather.6.cloned.1.call-update) | async-done | bytes 10223632 | tf_op jit(solution)/shard_map/all_gather | solution.py:45
  126.5 13.7 %reshape.174 = bf16[16,319488]{1,0:T(8,128)(2,1)} reshape(bf16[5111808]{0:T(1024)(128)(2,1)} %all-gather.6.cloned.1.call-done) | data formatting | bytes 20447232 | tf_op jit(solution)/shard_map/all_gather | solution.py:45
  140.2 5.1 %fusion.54 = (bf16[16,131072]{1,0:T(8,128)(2,1)S(1)}, bf16[16,131072]{1,0:T(8,128)(2,1)}) fusion(bf16[16,319488]{1,0:T(8,128)(2,1)} %reshape.174), kind=kLoop, calls=%fused_computation.89 | loop fusion | bytes 16777216 | tf_op jit(solution)/shard_map/slice | solution.py:47
  145.3 2.9 copy.90
  148.1 6.4 %copy.68 = bf16[512,16,256]{0,2,1:T(8,128)(2,1)} copy(bf16[512,16,256]{2,0,1:T(8,128)(2,1)} %bitcast.91) | data formatting | bytes 8388608 | tf_op jit(solution)/shard_map/transpose | solution.py:40
  154.6 1.6 fusion.55
  156.6 3.6 convolution_convert_fusion.9
  160.7 7.7 %convolution_convert_fusion.3 = bf16[3072,512]{0,1:T(8,128)(2,1)} fusion(bf16[3072,896]{1,0:T(8,128)(2,1)} %bitcast.2, bf16[896,512]{1,0:T(8,128)(2,1)S(1)} %reshape_reshape.15), kind=kOutput, calls=%fused_computation.12 | convolution fusion | flops 2820145152 | bytes 9568256 | tf_op jit(solution)/shard_map/dot_general | solution.py:116
  168.4 7.4 %convolution_convert_fusion.4 = bf16[3072,512]{0,1:T(8,128)(2,1)} fusion(bf16[3072,896]{1,0:T(8,128)(2,1)} %bitcast.2, bf16[896,512]{1,0:T(8,128)(2,1)S(1)} %reshape_reshape.13), kind=kOutput, calls=%fused_computation.13 | convolution fusion | flops 2820145152 | bytes 9568256 | tf_op jit(solution)/shard_map/dot_general | solution.py:117
  175.9 5.1 %reshape_reshape.14 = bf16[4096,512]{1,0:T(8,128)(2,1)} reshape(bf16[16,131072]{1,0:T(8,128)(2,1)} %get-tuple-element.43) | data formatting | bytes 8388608 | tf_op jit(solution)/shard_map/reshape;reshape | solution.py:40
  180.9 3.3 convolution_convert_fusion.10
  184.3 5.6 %fusion.58 = f32[4,128,3072]{2,1,0:T(8,128)} fusion(bf16[128,4,128]{0,2,1:T(8,128)(2,1)S(1)} %bitcast.103, bf16[3072,4,128]{0,2,1:T(8,128)(2,1)} %bitcast.93), kind=kOutput, calls=%fused_computation.93 | convolution fusion | flops 402653184 | bytes 9568256 | tf_op jit(solution)/shard_map/thd,khd->htk/dot_general | solution.py:139
  189.9 7.0 %fusion.57 = (f32[4,128]{1,0:T(4,128)S(1)}, f32[4,128,3072]{2,1,0:T(8,128)}) fusion(pred[128,3072]{1,0:T(8,128)(4,1)S(1)} %broadcast_compare_fusion, bf16[128,4,128]{0,2,1:T(8,128)(2,1)S(1)} %bitcast.111, bf16[3072,4,128]{0,2,1:T(8,128)(2,1)} %bitcast.121), kind=kOutput, calls=%fused_computation.92 | convolution fusion | flops 408947712 | bytes 9963520 | tf_op jit(solution)/shard_map/sub | solution.py:129
  196.9 5.5 %convolution_convert_fusion.5 = bf16[4,128,3072]{2,1,0:T(8,128)(2,1)} fusion(bf16[128,4,128]{0,2,1:T(8,128)(2,1)S(1)} %bitcast.104, f32[4,128,3072]{2,1,0:T(8,128)} %get-tuple-element.55, f32[4,128]{1,0:T(4,128)S(1)} %get-tuple-element.54), kind=kOutput, calls=%fused_computation.14 | convolution fusion | flops 407371776 | bytes 9570304 | tf_op jit(solution)/shard_map/htk,thd->khd/dot_general | solution.py:146
  202.3 12.1 %convolution_convert_fusion.6 = bf16[4,128,3072]{2,1,0:T(8,128)(2,1)} fusion(bf16[128,4,128]{0,2,1:T(8,128)(2,1)S(1)} %bitcast.112, f32[4,128,3072]{2,1,0:T(8,128)} %fusion.58, f32[4,128,3072]{2,1,0:T(8,128)} %get-tuple-element.55, f32[4,128]{1,0:T(4,128)S(1)} %get-tuple-element.54), kind=kOutput, calls=%fused_computation.15 | convolution fusion | flops 415239680 | bytes 15861760 | tf_op jit(solution)/shard_map/htk,thd->khd/dot_general | solution.py:144
  214.4 7.1 %convolution_convert_fusion.8 = bf16[896,512]{0,1:T(8,128)(2,1)S(1)} fusion(bf16[3072,512]{0,1:T(8,128)(2,1)} %bitcast.119, bf16[3072,896]{1,0:T(8,128)(2,1)} %bitcast.2), kind=kOutput, calls=%fused_computation.39 | convolution fusion | flops 2819031040 | bytes 9568256 | tf_op jit(solution)/shard_map/dot_general | solution.py:157
  221.5 6.0 %convolution_convert_fusion.7 = bf16[896,512]{0,1:T(8,128)(2,1)S(1)} fusion(bf16[3072,512]{0,1:T(8,128)(2,1)S(1)} %bitcast.118, bf16[3072,896]{1,0:T(8,128)(2,1)} %bitcast.2), kind=kOutput, calls=%fused_computation.38 | convolution fusion | flops 2819031040 | bytes 9568256 | tf_op jit(solution)/shard_map/dot_general | solution.py:158
  227.5 1.4 pad_maximum_fusion
  229.2 4.8 %fusion.27 = bf16[4,128,128]{2,1,0:T(8,128)(2,1)S(1)} fusion(bf16[3072,4,128]{0,2,1:T(8,128)(2,1)} %bitcast.94, f32[4,128,3072]{2,1,0:T(8,128)} %get-tuple-element.55, f32[4,128]{1,0:T(4,128)S(1)} %get-tuple-element.54), kind=kOutput, calls=%fused_computation.45 | convolution fusion | flops 405864448 | bytes 9570304 | tf_op jit(solution)/shard_map/htk,khd->thd/dot_general | solution.py:132
  234.0 4.4 %convolution_convert_fusion = bf16[512,4096]{1,0:T(8,128)(2,1)} fusion(bf16[128,512]{0,1:T(8,128)(2,1)S(1)} %bitcast.105, bf16[4096,257]{0,1:T(8,128)(2,1)} %all-gather.4.cloned.1.call-done), kind=kOutput, calls=%fused_computation.8 | convolution fusion | flops 538968064 | bytes 5373952 | tf_op jit(solution)/shard_map/dot_general | solution.py:148
  238.4 11.7 %fusion.30 = bf16[4,128,128]{2,1,0:T(8,128)(2,1)S(1)} fusion(bf16[3072,4,128]{0,2,1:T(8,128)(2,1)} %bitcast.122, f32[4,128,3072]{2,1,0:T(8,128)} %fusion.58, f32[4,128,3072]{2,1,0:T(8,128)} %get-tuple-element.55, f32[4,128]{1,0:T(4,128)S(1)} %get-tuple-element.54), kind=kOutput, calls=%fused_computation.46 | convolution fusion | flops 413732352 | bytes 15861760 | tf_op jit(solution)/shard_map/htk,khd->thd/dot_general | solution.py:142
  250.1 3.8 convolution_convert_fusion.1
  255.0 4.3 %all-to-all-start.3 = ((bf16[4,128,1024]{2,1,0:T(8,128)(2,1)}), bf16[4,128,1024]{2,1,0:T(8,128)(2,1)S(1)}, u32[]{:S(2)}, u32[]{:S(2)}) async-start(bf16[4,128,1024]{2,1,0:T(8,128)(2,1)} %bitcast.86), calls=%async_computation.3 | async-start | bytes 2097152 | tf_op jit(solution)/shard_map/all_to_all | solution.py:66
  259.3 3.7 convolution_convert_fusion.2
  263.0 1.2 copy.94
  264.1 10.2 %all-to-all-done.3 = bf16[4,128,1024]{2,1,0:T(8,128)(2,1)S(1)} async-done(((bf16[4,128,1024]{2,1,0:T(8,128)(2,1)}), bf16[4,128,1024]{2,1,0:T(8,128)(2,1)S(1)}, u32[]{:S(2)}, u32[]{:S(2)}) %all-to-all-start.3) | async-done | bytes 1048608 | tf_op jit(solution)/shard_map/all_to_all | solution.py:66
  274.3 3.5 all-to-all-start.2
  277.8 9.8 %fusion.59 = f32[3072,896]{1,0:T(8,128)} fusion(bf16[3072,512]{0,1:T(8,128)(2,1)} %bitcast.120, bf16[896,512]{1,0:T(8,128)(2,1)} %copy-done.5), kind=kOutput, calls=%fused_computation.94 | convolution fusion | flops 2818572288 | bytes 15073280 | tf_op jit(solution)/shard_map/dot_general | solution.py:168
  288.0 3.9 all-to-all-done.2
  292.5 3.5 all-to-all-start.4
  296.0 11.2 %add_convert_fusion = bf16[3072,896]{1,0:T(8,128)(2,1)} fusion(f32[3072,896]{1,0:T(8,128)} %fusion.59, bf16[3072,512]{0,1:T(8,128)(2,1)} %bitcast.117, bf16[896,512]{1,0:T(8,128)(2,1)} %copy-done.4), kind=kOutput, calls=%fused_computation.2 | convolution fusion | flops 2824077312 | bytes 20578304 | tf_op jit(solution)/shard_map/dot_general | solution.py:168
  307.3 5.2 %all-to-all-start.5 = ((bf16[4,6,128,896]{3,2,1,0:T(8,128)(2,1)}), bf16[4,6,128,896]{3,2,1,0:T(8,128)(2,1)}, u32[]{:S(2)}, u32[]{:S(2)}) async-start(bf16[4,6,128,896]{3,2,1,0:T(8,128)(2,1)} %bitcast.95), calls=%async_computation.5 | async-start | bytes 11010048 | tf_op jit(solution)/shard_map/all_to_all | solution.py:66
  315.1 3.1 all-reduce.3.cloned.1.call-done
  318.2 1.2 dynamic-slice_convert_fusion
  320.9 52.6 %all-to-all-done.5 = bf16[4,6,128,896]{3,2,1,0:T(8,128)(2,1)} async-done(((bf16[4,6,128,896]{3,2,1,0:T(8,128)(2,1)}), bf16[4,6,128,896]{3,2,1,0:T(8,128)(2,1)}, u32[]{:S(2)}, u32[]{:S(2)}) %all-to-all-start.5) | async-done | bytes 5505056 | tf_op jit(solution)/shard_map/all_to_all | solution.py:66
  373.5 4.9 %reduce_sum.112 = bf16[6,128,896]{2,1,0:T(8,128)(2,1)} reduce(bf16[4,6,128,896]{3,2,1,0:T(8,128)(2,1)} %all-to-all-done.5, bf16[]{:T(256)} %constant.53.clone.1), dimensions={0}, to_apply=%region_11.12 | reduce | flops 2064384 | bytes 6881282 | tf_op jit(solution)/shard_map/reduce_sum | solution.py:67
  378.5 19.8 %reduce-scatter.3.cloned.1.call-done = bf16[512,256]{1,0:T(8,128)(2,1)} async-done(((bf16[512,4096]{1,0:T(8,128)(2,1)}), bf16[512,256]{1,0:T(8,128)(2,1)}) %reduce-scatter.3.cloned.1.call-update) | async-done | bytes 262160 | tf_op jit(solution)/shard_map/reduce_scatter | solution.py:149
  398.3 1.8 convert_element_type.187
  (76 shorter events, 16.2 us)
Async XLA Ops:
  7.2 13.0 %copy-start = (bf16[1024,896]{1,0:T(8,128)(2,1)S(1)}, bf16[1024,896]{1,0:T(8,128)(2,1)}, u32[]{:S(2)}) copy-start(bf16[1024,896]{1,0:T(8,128)(2,1)} %param.18) | copy-start | bytes 5505028
  7.2 7.7 %copy-start.2 = (bf16[128,1024]{1,0:T(8,128)(2,1)S(1)}, bf16[128,1024]{1,0:T(8,128)(2,1)}, u32[]{:S(2)}) copy-start(bf16[128,1024]{1,0:T(8,128)(2,1)} %param.12) | copy-start | bytes 786436
  7.2 11.7 %copy-start.11 = (s32[24]{0:T(128)S(1)}, s32[24]{0:T(128)}, u32[]{:S(2)}) copy-start(s32[24]{0:T(128)} %param.15) | copy-start | bytes 292
  7.2 39.4 %all-gather.4.cloned.1.call-start = ((), (), s32[]{:S(2)}) async-start(), calls=%async_computation.7 | async-start | bytes 2703360 | tf_op jit(solution)/shard_map/all_gather | solution.py:14
  10.0 16.0 %copy-start.7 = (bf16[896]{0:T(1024)(128)(2,1)S(1)}, bf16[896]{0:T(1024)(128)(2,1)}, u32[]{:S(2)}) copy-start(bf16[896]{0:T(1024)(128)(2,1)} %param.17) | copy-start | bytes 5380
  10.0 116.5 %all-gather.6.cloned.1.call-start = ((), (), s32[]{:S(2)}) async-start(), calls=%async_computation.9 | async-start | bytes 10862592 | tf_op jit(solution)/shard_map/all_gather | solution.py:45
  15.0 5.2 %collective-permute-start = (bf16[1,1024]{1,0:T(2,128)(2,1)S(1)}, bf16[1,1024]{1,0:T(2,128)(2,1)S(1)}, u32[]{:S(2)}, u32[]{:S(2)}) collective-permute-start(bf16[1,1024]{1,0:T(2,128)(2,1)S(1)} %get-tuple-element.50), channel_id=1, source_target_pairs={{0,8},{8,16},{16,24},{24,32},{32,40},{40,48},{48,56},{56,64},{64,7... | collective-permute-start | bytes 6152 | tf_op jit(solution)/shard_map/ppermute | solution.py:25
  21.2 10.2 %all-to-all-start = ((f32[4,2,896]{2,1,0:T(2,128)}), f32[4,2,896]{2,1,0:T(2,128)S(1)}, u32[]{:S(2)}, u32[]{:S(2)}) async-start(f32[4,2,896]{2,1,0:T(2,128)} %broadcast_in_dim.20), calls=%async_computation | async-start | bytes 57344 | tf_op jit(solution)/shard_map/all_to_all | solution.py:30
  40.9 119.8 %all-to-all-start.1 = ((bf16[4,6,128,896]{3,2,1,0:T(8,128)(2,1)}), bf16[4,6,128,896]{3,2,1,0:T(8,128)(2,1)}, u32[]{:S(2)}, u32[]{:S(2)}) async-start(bf16[4,6,128,896]{3,2,1,0:T(8,128)(2,1)} %broadcast_in_dim.21), calls=%async_computation.1 | async-start | bytes 11010048 | tf_op jit(solution)/shard_map/all_to_all | solution.py:30
  46.1 272.2 %all-reduce.3.cloned.1.call-start = ((), (), s32[]{:S(2)}) async-start(), calls=%async_computation.10 | async-start | bytes 3670016
  156.6 4.1 %copy-start.5 = (bf16[896,512]{1,0:T(8,128)(2,1)}, bf16[896,512]{1,0:T(8,128)(2,1)S(1)}, u32[]{:S(2)}) copy-start(bf16[896,512]{1,0:T(8,128)(2,1)S(1)} %reshape_reshape.15) | copy-start | bytes 2752516
  160.7 7.7 %copy-start.4 = (bf16[896,512]{1,0:T(8,128)(2,1)}, bf16[896,512]{1,0:T(8,128)(2,1)S(1)}, u32[]{:S(2)}) copy-start(bf16[896,512]{1,0:T(8,128)(2,1)S(1)} %reshape_reshape.13) | copy-start | bytes 2752516
  175.9 5.1 %copy-start.9 = (f32[128]{0:T(128)S(1)}, f32[128]{0:T(128)}, u32[]{:S(2)}) copy-start(f32[128]{0:T(128)} %get-tuple-element.53) | copy-start | bytes 1540
  214.4 7.1 %copy-start.12 = (bf16[4,128,3072]{2,1,0:T(8,128)(2,1)S(1)}, bf16[4,128,3072]{2,1,0:T(8,128)(2,1)}, u32[]{:S(2)}) copy-start(bf16[4,128,3072]{2,1,0:T(8,128)(2,1)} %convolution_convert_fusion.5) | copy-start | bytes 9437188
  228.9 169.4 %reduce-scatter.3.cloned.1.call-start = ((), (), s32[]{:S(2)}) async-start(), calls=%async_computation.8 | async-start | bytes 4456448 | tf_op jit(solution)/shard_map/reduce_scatter | solution.py:149
  253.9 5.4 %copy-start.6 = (bf16[1024]{0:T(1024)(128)(2,1)S(1)}, bf16[1024]{0:T(1024)(128)(2,1)}, u32[]{:S(2)}) copy-start(bf16[1024]{0:T(1024)(128)(2,1)} %param.16) | copy-start | bytes 6148
  255.0 19.3 %all-to-all-start.3 = ((bf16[4,128,1024]{2,1,0:T(8,128)(2,1)}), bf16[4,128,1024]{2,1,0:T(8,128)(2,1)S(1)}, u32[]{:S(2)}, u32[]{:S(2)}) async-start(bf16[4,128,1024]{2,1,0:T(8,128)(2,1)} %bitcast.86), calls=%async_computation.3 | async-start | bytes 2097152 | tf_op jit(solution)/shard_map/all_to_all | solution.py:66
  274.3 17.6 %all-to-all-start.2 = ((bf16[4,128,1024]{2,1,0:T(8,128)(2,1)}), bf16[4,128,1024]{2,1,0:T(8,128)(2,1)S(1)}, u32[]{:S(2)}, u32[]{:S(2)}) async-start(bf16[4,128,1024]{2,1,0:T(8,128)(2,1)} %bitcast.96), calls=%async_computation.2 | async-start | bytes 2097152 | tf_op jit(solution)/shard_map/all_to_all | solution.py:66
  292.5 14.7 %all-to-all-start.4 = ((f32[4,128,1]{1,2,0:T(1,128)}), f32[4,128,1]{1,2,0:T(1,128)S(1)}, u32[]{:S(2)}, u32[]{:S(2)}) async-start(f32[4,128,1]{1,2,0:T(1,128)} %broadcast_in_dim.25), calls=%async_computation.4 | async-start | bytes 4096 | tf_op jit(solution)/shard_map/all_to_all | solution.py:30
  307.2 5.3 %copy-start.13 = (u32[128]{0:T(128)S(1)}, u32[128]{0:T(128)}, u32[]{:S(2)}) copy-start(u32[128]{0:T(128)} %constant.60) | copy-start | bytes 1540
  307.2 6.7 %copy-start.3 = (bf16[128,1024]{1,0:T(8,128)(2,1)S(1)}, bf16[128,1024]{1,0:T(8,128)(2,1)}, u32[]{:S(2)}) copy-start(bf16[128,1024]{1,0:T(8,128)(2,1)} %param.13) | copy-start | bytes 786436
  307.2 6.7 %copy-start.8 = (f32[128]{0:T(128)S(1)}, f32[128]{0:T(128)}, u32[]{:S(2)}) copy-start(f32[128]{0:T(128)} %get-tuple-element.52) | copy-start | bytes 1540
  307.2 6.7 %copy-start.10 = (f32[128]{0:T(128)S(1)}, f32[128]{0:T(128)}, u32[]{:S(2)}) copy-start(f32[128]{0:T(128)} %get-tuple-element.53) | copy-start | bytes 1540
  307.3 66.3 %all-to-all-start.5 = ((bf16[4,6,128,896]{3,2,1,0:T(8,128)(2,1)}), bf16[4,6,128,896]{3,2,1,0:T(8,128)(2,1)}, u32[]{:S(2)}, u32[]{:S(2)}) async-start(bf16[4,6,128,896]{3,2,1,0:T(8,128)(2,1)} %bitcast.95), calls=%async_computation.5 | async-start | bytes 11010048 | tf_op jit(solution)/shard_map/all_to_all | solution.py:66
  320.2 79.9 %copy-start.1 = (bf16[1024,896]{1,0:T(8,128)(2,1)S(1)}, bf16[1024,896]{1,0:T(8,128)(2,1)}, u32[]{:S(2)}) copy-start(bf16[1024,896]{1,0:T(8,128)(2,1)} %param.18) | copy-start | bytes 5505028
Sparse Core Ops, SparseCore 0:
  10.1 34.1 all-gather.3
  47.1 79.3 all-gather.5
  229.0 89.1 all-reduce.2
  321.4 76.8 reduce-scatter.2
where the time goes:
time: 412 us; the launch traced here: 407 us
  waiting for transfers between devices  173 us (42%)
  matrix products  119 us (29%)
  local copies, waits for them, and re-layouts  49.6 us (12%)
  starting transfers between devices  30.9 us (8%)
  other arithmetic  18.8 us (5%)
  between operations  15.1 us (4%)
    all_gather x1, waiting for transfers between devices, one_gather(): lines, at, done = (lax.all_gather(vector, axis), 0, [])  76.9 us
    all_to_all x3, waiting for transfers between devices, sent_and_summed(): lax.all_to_all(parts, axis, split_axis=0, concat_axis=0, tiled=True)  66.7 us
    reduce_scatter x1, waiting for transfers between devices, body(): lax.psum_scatter(wo_partial.astype(jnp.bfloat16), 'seq', scatter_dimensio...  19.8 us
    all_gather x1, local copies, waits for them, and re-layouts, one_gather(): lines, at, done = (lax.all_gather(vector, axis), 0, [])  13.7 us
    all_to_all x3, starting transfers between devices, sent_and_summed(): lax.all_to_all(parts, axis, split_axis=0, concat_axis=0, tiled=True)  13 us
    all_to_all x3, starting transfers between devices, sent_to_all(): return lax.all_to_all(copies, axis, split_axis=0, concat_axis=0, tiled=True)  13 us
    dot_general x1, matrix products, body(): jnp.einsum('htk,thd->khd', d_scores, query3, preferred_element_type=single)  12.1 us
    dot_general x1, matrix products, body(): jnp.einsum('htk,khd->thd', d_scores, keys3, preferred_element_type=single)  11.7 us
  transfers between devices with their start and end apart: 11, of which 8 were waited for; matrix products, arithmetic and copies ran while one was open for 28% of the time, Pallas kernels for 0%

commit v1 on v0

v1 whole, which is shorter than its diff:
```python
import functools

import jax
import jax.numpy as jnp
from jax import lax
from jax.experimental import pallas as pl
from jax.experimental.pallas import tpu as pltpu
from jax.sharding import PartitionSpec as P

HD = 128
CLEN = 64
NLEN = 128
KMAX = 8
F32 = jnp.float32
BF16 = jnp.bfloat16
VMEM = pl.BlockSpec(memory_space=pltpu.VMEM)
SMEM = pl.BlockSpec(memory_space=pltpu.SMEM)


def dot(a, b, dims=((1,), (0,))):
    return lax.dot_general(a, b, (dims, ((), ())), preferred_element_type=F32)


NT = ((1,), (1,))
TN = ((0,), (0,))


def shift(x, by):
    n = lax.axis_size("nbr")
    return lax.ppermute(x, "nbr", [(i, (i + by) % n) for i in range(n)])


def ring_gather(x):
    half = x.shape[0] // 2
    right = shift(x, -1)
    left = shift(x, 1)
    far_a = shift(right[:half], -1)
    far_b = shift(left[half:], 1)
    return x, right, (far_a, far_b), left


def ring_scatter(parts):
    own, to_right, to_far, to_left = parts
    half = own.shape[0] // 2
    via_left = shift(to_far[:half], 1)
    via_right = shift(to_far[half:], -1)
    plain_left = shift(to_right[half:], 1)
    plain_right = shift(to_left[:half], -1)
    sum_right = (to_right[:half].astype(F32) + via_left.astype(F32)).astype(BF16)
    sum_left = (to_left[half:].astype(F32) + via_right.astype(F32)).astype(BF16)
    summed_left = shift(sum_right, 1)
    summed_right = shift(sum_left, -1)
    low = own[:half].astype(F32) + summed_left.astype(F32) + plain_right.astype(F32)
    high = own[half:].astype(F32) + plain_left.astype(F32) + summed_right.astype(F32)
    return low, high


def sum_small(x):
    return x + shift(x, 1) + shift(x, 2) + shift(x, 3)


def rms_scale(values):
    return lax.rsqrt(jnp.mean(values * values, axis=-1, keepdims=True) + 1e-06)


def project_kernel(n_ref, x_ref, d_ref, w_ref, q_ref, dc_ref, qa, da):
    step = pl.program_id(0)
    x, d, w = x_ref[0], d_ref[0], w_ref
    q = jnp.zeros(qa.shape, F32)
    dc = jnp.zeros(da.shape, F32)
    for s in range(4):
        wq = w[2 * s : 2 * s + 2, 0:128, :].reshape(256, 512)
        wo = w[2 * s : 2 * s + 2, 128:256, :].reshape(256, 512)
        q += dot(x[:, 256 * s : 256 * s + 256], wq)
        dc += dot(d[:, 256 * s : 256 * s + 256], wo)

    @pl.when(step == 0)
    def _():
        qa[...] = q
        da[...] = dc

    @pl.when(step > 0)
    def _():
        qa[...] += q
        da[...] += dc

    @pl.when(step == 3)
    def _():
        q_ref[...] = qa[...].astype(BF16)
        dc_ref[...] = da[...].astype(BF16)


def project(n, normed, dout, weights):
    tokens = normed.shape[1]
    return pl.pallas_call(
        project_kernel,
        grid_spec=pltpu.PrefetchScalarGridSpec(
            num_scalar_prefetch=1,
            grid=(4,),
            in_specs=[
                pl.BlockSpec((1, tokens, 1024), lambda r, n: (r, 0, 0)),
                pl.BlockSpec((1, tokens, 1024), lambda r, n: (r, 0, 0)),
                pl.BlockSpec((8, 256, 512), lambda r, n: ((n[0] + r) % 4, 0, 0)),
            ],
            out_specs=[
                pl.BlockSpec((tokens, 512), lambda r, n: (0, 0)),
                pl.BlockSpec((tokens, 512), lambda r, n: (0, 0)),
            ],
            scratch_shapes=[pltpu.VMEM((tokens, 512), F32)] * 2,
        ),
        out_shape=[jax.ShapeDtypeStruct((tokens, 512), BF16)] * 2,
        compiler_params=pltpu.CompilerParams(vmem_limit_bytes=32 << 20),
        name="project",
    )(n, normed, dout, weights)


def attend_kernel(tab, e0, e1, e2a, e2b, e3, wk, wv, q, dc, enc, ctx, dq, dk, dv, kb, vb):
    half = e2a.shape[0]
    tables = ((e0, 0), (e1, 6), (e2a, 12), (e2b, 12 + half), (e3, 18))

    def pick(j, carry):
        src = tab[j]

        @pl.when(src < 0)
        def _():
            enc[j] = jnp.zeros(enc.shape[1:], BF16)

        for ref, first in tables:

            @pl.when((src >= first) & (src < first + ref.shape[0]))
            def _(ref=ref, first=first):
                enc[j] = ref[src - first]

        return carry

    lax.fori_loop(0, 2 * KMAX, pick, 0)

    def kv(c, carry):
        x = enc[pl.ds(4 * c, 4)].reshape(4 * NLEN, enc.shape[2])
        rows = pl.ds(pl.multiple_of(c * 512, 512), 512)
        kb[rows, :] = dot(x, wk[...]).astype(BF16)
        vb[rows, :] = dot(x, wv[...]).astype(BF16)
        return carry

    lax.fori_loop(0, 4, kv, 0)
    factor = HD ** (-0.5)
    heads = q.shape[1] // HD
    keys = KMAX * NLEN
    for c in range(2):
        limit = tab[2 * KMAX + c] * NLEN
        allowed = lax.broadcasted_iota(jnp.int32, (CLEN, keys), 1) < limit
        toks = slice(c * CLEN, (c + 1) * CLEN)
        rows = slice(c * keys, (c + 1) * keys)
        for h in range(heads):
            cols = slice(h * HD, (h + 1) * HD)
            qh, dh = q[toks, cols], dc[toks, cols]
            kh, vh = kb[rows, cols], vb[rows, cols]
            s = jnp.where(allowed, dot(qh, kh, NT) * factor, -1e30)
            w = jnp.exp(s - jnp.max(s, axis=-1, keepdims=True))
            p = w / jnp.sum(w, axis=-1, keepdims=True)
            pb = p.astype(BF16)
            ctx[toks, cols] = dot(pb, vh).astype(BF16)
            dp = dot(dh, vh, NT)
            rd = jnp.sum(p * dp, axis=-1, keepdims=True)
            ds = (p * (dp - rd) * factor).astype(BF16)
            dq[toks, cols] = dot(ds, kh).astype(BF16)
            dk[rows, cols] = dot(ds, qh, TN).astype(BF16)
            dv[rows, cols] = dot(pb, dh, TN).astype(BF16)


def attend(tab, blocks, wk, wv, q, dc):
    width = wk.shape[0]
    rows = 2 * KMAX * NLEN
    flat = jax.ShapeDtypeStruct((rows, q.shape[1]), BF16)
    same = jax.ShapeDtypeStruct(q.shape, BF16)
    return pl.pallas_call(
        attend_kernel,
        in_specs=[SMEM] + [VMEM] * 9,
        out_specs=[VMEM] * 5,
        out_shape=[jax.ShapeDtypeStruct((2 * KMAX, NLEN, width), BF16), same, same, flat, flat],
        scratch_shapes=[pltpu.VMEM((rows, q.shape[1]), BF16)] * 2,
        compiler_params=pltpu.CompilerParams(vmem_limit_bytes=48 << 20),
        name="attend",
    )(tab, *blocks, wk, wv, q, dc)


def spread_kernel(inv, dk, dv, wk, wv, o0, o1, o2, o3, de):
    def grad(c, carry):
        rows = pl.ds(pl.multiple_of(c * 512, 512), 512)
        part = dot(dk[rows, :], wk[...], NT) + dot(dv[rows, :], wv[...], NT)
        de[pl.ds(4 * c, 4)] = part.astype(BF16).reshape(4, NLEN, wk.shape[0])
        return carry

    lax.fori_loop(0, 4, grad, 0)

    def place(i, carry):
        for r, out in enumerate((o0, o1, o2, o3)):
            src = inv[r * 6 + i]

            @pl.when(src < 0)
            def _(out=out):
                out[i] = jnp.zeros(out.shape[1:], BF16)

            @pl.when(src >= 0)
            def _(out=out, src=src):
                out[i] = de[src]

        return carry

    lax.fori_loop(0, 6, place, 0)


def spread(inv, dk, dv, wk, wv):
    width = wk.shape[0]
    return pl.pallas_call(
        spread_kernel,
        in_specs=[SMEM] + [VMEM] * 4,
        out_specs=[VMEM] * 4,
        out_shape=[jax.ShapeDtypeStruct((6, NLEN, width), BF16)] * 4,
        scratch_shapes=[pltpu.VMEM((2 * KMAX, NLEN, width), BF16)],
        compiler_params=pltpu.CompilerParams(vmem_limit_bytes=48 << 20),
        name="spread",
    )(inv, dk, dv, wk, wv)


def unproject_kernel(n_ref, ctx, dq, w, o):
    for s in range(4):
        wq = w[2 * s : 2 * s + 2, 0:128, :].reshape(256, 512)
        wo = w[2 * s : 2 * s + 2, 128:256, :].reshape(256, 512)
        o[0, 0, :, 256 * s : 256 * s + 256] = dot(ctx[...], wo, NT).astype(BF16)
        o[0, 1, :, 256 * s : 256 * s + 256] = dot(dq[...], wq, NT).astype(BF16)


def unproject(n, ctx, dq, weights):
    tokens = ctx.shape[0]
    return pl.pallas_call(
        unproject_kernel,
        grid_spec=pltpu.PrefetchScalarGridSpec(
            num_scalar_prefetch=1,
            grid=(4,),
            in_specs=[
                pl.BlockSpec((tokens, 512), lambda r, n: (0, 0)),
                pl.BlockSpec((tokens, 512), lambda r, n: (0, 0)),
                pl.BlockSpec((8, 256, 512), lambda r, n: ((n[0] + r) % 4, 0, 0)),
            ],
            out_specs=pl.BlockSpec((1, 2, tokens, 1024), lambda r, n: (r, 0, 0, 0)),
        ),
        out_shape=jax.ShapeDtypeStruct((4, 2, tokens, 1024), BF16),
        compiler_params=pltpu.CompilerParams(vmem_limit_bytes=32 << 20),
        name="unproject",
    )(n, ctx, dq, weights)


def outer_kernel(n_ref, d, ctx, o):
    for s in range(4):
        o[s] = dot(d[0, :, 256 * s : 256 * s + 256], ctx[...], TN).astype(BF16)


def outer(n, dout, ctx):
    tokens = ctx.shape[0]
    return pl.pallas_call(
        outer_kernel,
        grid_spec=pltpu.PrefetchScalarGridSpec(
            num_scalar_prefetch=1,
            grid=(4,),
            in_specs=[
                pl.BlockSpec((1, tokens, 1024), lambda r, n: (r, 0, 0)),
                pl.BlockSpec((tokens, 512), lambda r, n: (0, 0)),
            ],
            out_specs=pl.BlockSpec((4, 256, 512), lambda r, n: ((n[0] + r) % 4, 0, 0)),
        ),
        out_shape=jax.ShapeDtypeStruct((16, 256, 512), BF16),
        compiler_params=pltpu.CompilerParams(vmem_limit_bytes=32 << 20),
        name="outer",
    )(n, dout, ctx)


def slot_tables(slot_span, n):
    rel = jnp.roll(slot_span.reshape(4, 6), -n, axis=0).reshape(-1)
    slots = rel.shape[0]
    ids = jnp.arange(slots, dtype=jnp.int32)
    before = ids[None, :] < ids[:, None]
    rank = jnp.sum((rel[None, :] == rel[:, None]) & before, axis=1, dtype=jnp.int32)
    where = jnp.where(rel >= 0, rel * KMAX + rank, -1).astype(jnp.int32)
    spot = jnp.arange(2 * KMAX, dtype=jnp.int32)
    hit = where[None, :] == spot[:, None]
    source = jnp.sum(jnp.where(hit, ids[None, :] + 1, 0), axis=1, dtype=jnp.int32) - 1
    counts = jnp.sum(rel[None, :] == jnp.arange(2)[:, None], axis=1, dtype=jnp.int32)
    return jnp.concatenate([source, counts]), where, rel


def body(hidden, d_out, nbr_emb, slot_span, dec_gain, enc_gain, w_cond, w_enc, w_q, w_k, w_v, w_o):
    n = lax.axis_index("nbr")
    b = lax.axis_index("batch")
    n1 = n.astype(jnp.int32).reshape(1)
    tokens, feats = hidden.shape
    spans = tokens // CLEN

    q_half = lax.dynamic_slice_in_dim(w_q, b * 128, 128, axis=0)
    o_half = lax.dynamic_slice_in_dim(w_o, b * 128, 128, axis=1).T
    kv_half = jnp.where(b == 0, w_k, w_v)
    weights = lax.all_gather(
        jnp.concatenate([q_half, o_half, kv_half], axis=0), ("seq", "batch"), axis=0
    )

    pooled = jnp.mean(hidden.astype(F32).reshape(spans, CLEN, feats), axis=1).astype(BF16)
    length = lax.axis_size("seq")
    carried = lax.ppermute(
        pooled[spans - 1 :], "seq", [(i, i + 1) for i in range(length - 1)]
    )
    previous = jnp.concatenate([carried, pooled[: spans - 1]], axis=0)
    condition = sum_small(jnp.dot(previous, w_cond, preferred_element_type=F32))

    e0, e1, (e2a, e2b), e3 = ring_gather(nbr_emb)
    gain_rows = jnp.broadcast_to(dec_gain[None], (8, feats))
    state = jnp.concatenate([hidden, gain_rows, d_out], axis=0)
    right, left = shift(state, -1), shift(state, 1)
    far_h, far_d = shift(right[: tokens + 8], -1), shift(left[tokens + 8 :], 1)

    tab, inv, rel_span = slot_tables(slot_span, n)

    def encode(block, first):
        own = lax.slice_in_dim(rel_span, first, first + block.shape[0])
        own = own[:, None, None]
        cond = jnp.where(own == 0, condition[0], jnp.where(own == 1, condition[1], 0.0))
        x = block.astype(F32) + cond
        enc_normed = (x * rms_scale(x) * enc_gain.astype(F32)).astype(BF16)
        width = x.shape[2]
        mixed = jnp.dot(
            enc_normed.reshape(-1, width), w_enc, preferred_element_type=F32
        ).reshape(x.shape)
        return (x + jax.nn.silu(mixed)).astype(BF16)

    encoded = [
        encode(e0, 0), encode(e1, 6), encode(e2a, 12), encode(e2b, 15), encode(e3, 18)
    ]

    hid_rel = jnp.stack([hidden, right[:tokens], far_h[:tokens], left[:tokens]])
    gain_rel = jnp.stack([dec_gain, right[tokens], far_h[tokens], left[tokens]])
    dout_rel = jnp.stack([d_out, right[tokens + 8 :], far_d, left[tokens + 8 :]])
    hf = hid_rel.astype(F32)
    rstd = lax.rsqrt(jnp.mean(hf * hf, axis=(0, 2)) + 1e-06)[:, None]
    normed = (hf * rstd[None] * gain_rel.astype(F32)[:, None, :]).astype(BF16)

    pairs = weights.reshape(16, 2, 312, 512)
    wk = pairs[:, 0, 256:].reshape(-1, 512)
    wv = pairs[:, 1, 256:].reshape(-1, 512)

    query, d_ctx = project(n1, normed, dout_rel, weights)
    enc, ctx, d_query, d_key, d_value = attend(tab, encoded, wk, wv, query, d_ctx)

    rows = enc.reshape(-1, enc.shape[2])
    d_wo_part = outer(n1, dout_rel, ctx)
    d_wk_part = dot(rows, d_key, TN).astype(BF16).reshape(16, -1, 512)
    d_wv_part = dot(rows, d_value, TN).astype(BF16).reshape(16, -1, 512)
    grads = jnp.concatenate([d_wo_part, d_wk_part, d_wv_part], axis=1)
    grads = lax.psum_scatter(grads, "seq", scatter_dimension=0, tiled=False).astype(F32)
    d_wo = grads[:256].T
    d_wk = grads[256:312]
    d_wv = grads[312:368]

    both = unproject(n1, ctx, d_query, weights)
    out_sum, own_grad = ring_scatter([both[0], both[1], both[2], both[3]])
    d_enc_low, d_enc_high = ring_scatter(spread(inv, d_key, d_value, wk, wv))
    d_enc = jnp.concatenate([d_enc_low, d_enc_high], axis=0).astype(BF16)

    own = hidden.astype(F32)
    out = (own + out_sum[0]).astype(BF16)
    scaled = dec_gain.astype(F32) * own_grad[0]
    stat = sum_small(jnp.sum(own * scaled, axis=-1, keepdims=True) / (4 * feats))
    d_hidden = d_out.astype(F32) + rstd * scaled - own * rstd**3 * stat
    return (out, d_hidden.astype(BF16), d_enc, d_wo, d_wk, d_wv)


def solution(mesh):
    placed = (
        P(("batch", "seq"), "nbr"),
        P(("batch", "seq"), "nbr"),
        P(("batch", "seq", "nbr"), None, None),
        P(("batch", "seq")),
        P("nbr"),
        P(),
        P("nbr", None),
        P(),
        P("seq", "nbr"),
        P("seq", "nbr"),
        P("seq", "nbr"),
        P("nbr", "seq"),
    )
    return jax.shard_map(
        body,
        mesh=mesh,
        in_specs=placed,
        out_specs=(
            P(("batch", "seq"), "nbr"),
            P(("batch", "seq"), "nbr"),
            P(("batch", "seq", "nbr"), None, None),
            P(("batch", "nbr"), "seq"),
            P(("batch", "seq"), "nbr"),
            P(("batch", "seq"), "nbr"),
        ),
        check_vma=False,
    )
```

time: 412 us -> 248 us (0.60); the launches traced: 407 us -> 247 us
  matrix products: 119 us -> 24.3 us
  waiting for transfers between devices: 173 us -> 107 us
  Pallas kernels: 0 us -> 35.7 us
  local copies, waits for them, and re-layouts: 49.6 us -> 19.3 us
    ppermute x1 -> x27, waiting for transfers between devices: 1.22 us -> 107 us  [the longest x26 107 us: shift(): return lax.ppermute(x, 'nbr', [(i, (i + by) % n) for i in range(n)])]
    dot_general x19 -> x8, matrix products: 112 us -> 24.3 us  [the longest x5 17 us: encode(): jnp.dot(enc_normed.reshape(-1, width), w_enc, preferred_element_type=F32)]
    all_gather x2 -> x1, waiting for transfers between devices: 76.9 us -> 0.01 us  [body(): lax.all_gather(jnp.concatenate([q_half, o_half, kv_half], axis=0), ('seq'...]
    all_to_all x6 -> x0, waiting for transfers between devices: 72.1 us -> none  [the longest x3 66.7 us: sent_and_summed(): lax.all_to_all(parts, axis, split_axis=0, concat_axis=0, tiled=True)]
    pallas_call x0 -> x5, Pallas kernels: none -> 35.7 us  [the longest x1 18 us: attend(): pl.pallas_call(attend_kernel, in_specs=[SMEM] + [VMEM] * 9, out_specs=[VM...]
    all_to_all x6 -> x0, starting transfers between devices: 26.1 us -> none  [the longest x3 13 us: sent_and_summed(): lax.all_to_all(parts, axis, split_axis=0, concat_axis=0, tiled=True)]
    ppermute x1 -> x27, starting transfers between devices: 3.9 us -> 28.9 us  [the longest x26 25 us: shift(): return lax.ppermute(x, 'nbr', [(i, (i + by) % n) for i in range(n)])]
    reduce_scatter x1 -> x0, waiting for transfers between devices: 19.8 us -> none  [body(): lax.psum_scatter(wo_partial.astype(jnp.bfloat16), 'seq', scatter_dimensio...]
  transfers between devices with their start and end apart: 11 -> 29, of which waited for: 8 -> 17; matrix products, arithmetic and copies ran while one was open for 28% -> 12% of each run, Pallas kernels for 0% -> 5%
where the time goes in v1:
time: 248 us; the launch traced here: 247 us
  waiting for transfers between devices  107 us (43%)
  Pallas kernels  35.7 us (14%)
  starting transfers between devices  28.9 us (12%)
  matrix products  24.3 us (10%)
  local copies, waits for them, and re-layouts  19.3 us (8%)
  other arithmetic  17 us (7%)
  between operations  14.6 us (6%)
    ppermute x26, waiting for transfers between devices, shift(): return lax.ppermute(x, 'nbr', [(i, (i + by) % n) for i in range(n)])  107 us
    ppermute x26, starting transfers between devices, shift(): return lax.ppermute(x, 'nbr', [(i, (i + by) % n) for i in range(n)])  25 us
    pallas_call x1, Pallas kernels, attend(): pl.pallas_call(attend_kernel, in_specs=[SMEM] + [VMEM] * 9, out_specs=[VM...  18 us
    dot_general x5, matrix products, encode(): jnp.dot(enc_normed.reshape(-1, width), w_enc, preferred_element_type=F32)  17 us
    unnamed x44, local copies, waits for them, and re-layouts  12 us
    pallas_call x1, Pallas kernels, spread(): pl.pallas_call(spread_kernel, in_specs=[SMEM] + [VMEM] * 4, out_specs=[VM...  9.14 us
    dot_general x2, matrix products, dot(): return lax.dot_general(a, b, (dims, ((), ())), preferred_element_type=F32)  7.01 us
  transfers between devices with their start and end apart: 29, of which 17 were waited for; matrix products, arithmetic and copies ran while one was open for 12% of the time, Pallas kernels for 5%

profile of v1, /device:TPU:0, one launch (start us, length us, event | category | flops | bytes accessed | tf_op | source)
XLA Modules:
  0.0 247.3 jit_solution(11826197951171697745)
XLA Ops:
  11.1 3.2 %collective-permute-start.4 = (bf16[6,128,896]{2,1,0:T(8,128)(2,1)}, bf16[6,128,896]{2,1,0:T(8,128)(2,1)}, u32[]{:S(2)}, u32[]{:S(2)}) collective-permute-start(bf16[6,128,896]{2,1,0:T(8,128)(2,1)} %param.14), channel_id=1, source_target_pairs={{0,6},{2,0},{4,2},{6,4},{1,7},{3,1},{5,3},{7,5},{8,14},{10,8},{12,... | collective-permute-start | bytes 4128776 | tf_op jit(solution)/shard_map/ppermute | solution.py:30
  14.3 3.8 %collective-permute-start = (bf16[1,1024]{1,0:T(2,128)(2,1)S(1)}, bf16[1,1024]{1,0:T(2,128)(2,1)S(1)}, u32[]{:S(2)}, u32[]{:S(2)}) collective-permute-start(bf16[1,1024]{1,0:T(2,128)(2,1)S(1)} %get-tuple-element.80), channel_id=1, source_target_pairs={{0,8},{8,16},{16,24},{24,32},{32,40},{40,48},{48,56},{56,64},{64,7... | collective-permute-start | bytes 6152 | tf_op jit(solution)/shard_map/ppermute | solution.py:308
  19.8 3.2 %collective-permute-start.3 = (f32[2,896]{1,0:T(2,128)S(1)}, f32[2,896]{1,0:T(2,128)S(1)}, u32[]{:S(2)}, u32[]{:S(2)}) collective-permute-start(f32[2,896]{1,0:T(2,128)S(1)} %fusion.48), channel_id=1, source_target_pairs={{0,6},{2,0},{4,2},{6,4},{1,7},{3,1},{5,3},{7,5},{8,14},{10,8},{12,... | collective-permute-start | bytes 21512 | tf_op jit(solution)/shard_map/ppermute | solution.py:30
  24.1 20.1 %collective-permute-done.3 = f32[2,896]{1,0:T(2,128)S(1)} collective-permute-done((f32[2,896]{1,0:T(2,128)S(1)}, f32[2,896]{1,0:T(2,128)S(1)}, u32[]{:S(2)}, u32[]{:S(2)}) %collective-permute-start.3) | collective-permute-done | bytes 7200 | tf_op jit(solution)/shard_map/ppermute | solution.py:30
  45.2 1.4 collective-permute-done.2
  46.6 1.3 collective-permute-start.8
  48.5 3.1 %add_convert_fusion.2.e0 = bf16[6,128,896]{2,1,0:T(8,128)(2,1)} fusion(bf16[6,128,896]{2,1,0:T(8,128)(2,1)S(1)} %copy-done.14, bf16[896,896]{1,0:T(8,128)(2,1)S(1)} %copy-done.20, f32[896]{0:T(1024)S(1)} %convert_element_type.222, f32[6,128]{1,0:T(8,128)S(1)} %add_rsqrt_fusion.2, f32[6,896]{1,0:T(8,128)S(1)} %get-tuple-element.77), kind=kOutput, calls=%fused_computation.9 | convolution fusion | flops 1242071040 | bytes 4386304 | tf_op jit(solution)/shard_map/dot_general | solution.py:329
  51.6 7.7 %collective-permute-done.10 = bf16[264,1024]{1,0:T(8,128)(2,1)S(1)} collective-permute-done((bf16[264,1024]{1,0:T(8,128)(2,1)S(1)}, bf16[264,1024]{1,0:T(8,128)(2,1)S(1)}, u32[]{:S(2)}, u32[]{:S(2)}) %collective-permute-start.10) | collective-permute-done | bytes 540704 | tf_op jit(solution)/shard_map/ppermute | solution.py:30
  59.6 3.3 %collective-permute-start.9 = (bf16[136,1024]{1,0:T(8,128)(2,1)S(1)}, bf16[136,1024]{1,0:T(8,128)(2,1)S(1)}, u32[]{:S(2)}, u32[]{:S(2)}) collective-permute-start(bf16[136,1024]{1,0:T(8,128)(2,1)S(1)} %slice.229), channel_id=1, source_target_pairs={{0,6},{2,0},{4,2},{6,4},{1,7},{3,1},{5,3},{7,5},{8,14},{10,8},{12,... | collective-permute-start | bytes 835592 | tf_op jit(solution)/shard_map/ppermute | solution.py:30
  63.0 4.4 %collective-permute-done.11 = bf16[128,1024]{1,0:T(8,128)(2,1)S(1)} collective-permute-done((bf16[128,1024]{1,0:T(8,128)(2,1)S(1)}, bf16[128,1024]{1,0:T(8,128)(2,1)S(1)}, u32[]{:S(2)}, u32[]{:S(2)}) %collective-permute-start.11) | collective-permute-done | bytes 262176 | tf_op jit(solution)/shard_map/ppermute | solution.py:30
  68.4 1.2 slice.224
  69.5 3.4 %collective-permute-start.5 = (bf16[3,128,896]{2,1,0:T(8,128)(2,1)S(1)}, bf16[3,128,896]{2,1,0:T(8,128)(2,1)S(1)}, u32[]{:S(2)}, u32[]{:S(2)}) collective-permute-start(bf16[3,128,896]{2,1,0:T(8,128)(2,1)S(1)} %slice.224), channel_id=1, source_target_pairs={{0,6},{2,0},{4,2},{6,4},{1,7},{3,1},{5,3},{7,5},{8,14},{10,8},{12,... | collective-permute-start | bytes 2064392 | tf_op jit(solution)/shard_map/ppermute | solution.py:30
  74.3 1.8 multiply_reduce_fusion.1
  76.1 1.8 multiply_reduce_fusion
  77.9 5.1 %add_convert_fusion.1.e1 = bf16[6,128,896]{2,1,0:T(8,128)(2,1)} fusion(bf16[6,128,896]{2,1,0:T(8,128)(2,1)} %collective-permute-done.4, bf16[896,896]{1,0:T(8,128)(2,1)S(1)} %copy-done.20, f32[6,128]{1,0:T(8,128)S(1)} %add_rsqrt_fusion.1, f32[6,896]{1,0:T(8,128)S(1)} %get-tuple-element.76, f32[896]{0:T(1024)S(1)} %convert_element_type.222), kind=kOutput, calls=%fused_computation.5 | convolution fusion | flops 1242071040 | bytes 4386304 | tf_op jit(solution)/shard_map/dot_general | solution.py:329
  83.0 4.8 %add_convert_fusion.e3 = bf16[6,128,896]{2,1,0:T(8,128)(2,1)} fusion(bf16[6,128,896]{2,1,0:T(8,128)(2,1)} %collective-permute-done.6, bf16[896,896]{1,0:T(8,128)(2,1)S(1)} %copy-done.20, f32[6,128]{1,0:T(8,128)S(1)} %add_rsqrt_fusion, f32[6,896]{1,0:T(8,128)S(1)} %get-tuple-element.75, f32[896]{0:T(1024)S(1)} %convert_element_type.222), kind=kOutput, calls=%fused_computation.1 | convolution fusion | flops 1242071040 | bytes 4386304 | tf_op jit(solution)/shard_map/dot_general | solution.py:329
  87.8 2.2 collective-permute-done.7
  90.5 2.0 add_convert_fusion.8.e2a
  92.4 2.0 add_convert_fusion.7.e2b
  94.4 1.6 fusion.54
  96.0 4.6 %copy-done.2 = bf16[9984,512]{1,0:T(8,128)(2,1)S(1)} copy-done((bf16[9984,512]{1,0:T(8,128)(2,1)S(1)}, bf16[9984,512]{1,0:T(8,128)(2,1)}, u32[]{:S(2)}) %copy-start.2) | copy-done | bytes 10223640
  100.6 2.7 %project.1 = (bf16[128,512]{1,0:T(8,128)(2,1)S(1)}, bf16[128,512]{1,0:T(8,128)(2,1)S(1)}) custom-call(s32[1]{0:T(128)} %bitcast.n_ref, bf16[4,128,1024]{2,1,0:T(8,128)(2,1)S(1)} %fusion.2.x_ref, bf16[4,128,1024]{2,1,0:T(8,128)(2,1)S(1)} %pad_maximum_fusion.3.d_ref.d, bf16[32,312,512]{2,1,0:T(8,128)(2,1)S(1)} %bitcast.122), custom_call_target="tpu_custom_call" | custom-call | tf_op jit(solution)/shard_map/project/pallas_call | solution.py:95
  103.4 18.0 %attend.1 = (bf16[16,128,896]{2,1,0:T(8,128)(2,1)}, bf16[128,512]{1,0:T(8,128)(2,1)S(1)}, bf16[128,512]{1,0:T(8,128)(2,1)S(1)}, bf16[2048,512]{1,0:T(8,128)(2,1)}, bf16[2048,512]{1,0:T(8,128)(2,1)}) custom-call(s32[18]{0:T(128)S(1)} %pad_add_fusion.1.tab, bf16[6,128,896]{2,1,0:T(8,128)(2,1)S(1)} %copy-done.8, bf16[6,128,896]{2,1,0:T(8,128)(2,1)} %add_convert_fusion.1.e1, ...), custom_call_target="tpu_custom_call" | custom-call | tf_op jit(solution)/shard_map/attend/pallas_call | solution.py:176
  121.4 4.9 %convolution_convert_fusion = bf16[896,512]{1,0:T(8,128)(2,1)S(1)} fusion(bf16[2048,896]{1,0:T(8,128)(2,1)} %bitcast.135, bf16[2048,512]{1,0:T(8,128)(2,1)} %get-tuple-element.22.dv), kind=kOutput, calls=%fused_computation.28 | convolution fusion | flops 1879506944 | bytes 6684672 | tf_op jit(solution)/shard_map/dot_general | solution.py:21
  126.4 2.1 convolution_convert_fusion.1
  128.4 1.9 outer.1
  130.3 4.5 %pad_maximum_fusion = bf16[16,368,512]{2,1,0:T(8,128)(2,1)} fusion(bf16[16,56,512]{2,1,0:T(8,128)(2,1)S(1)} %bitcast.131, bf16[16,56,512]{2,1,0:T(8,128)(2,1)S(1)} %bitcast.132, bf16[16,256,512]{2,1,0:T(8,128)(2,1)S(1)} %outer.1), kind=kLoop, calls=%fused_computation | loop fusion | flops 18087936 | bytes 12058624 | tf_op jit(solution)/shard_map/concatenate | solution.py:356
  136.1 1.2 copy-done.7
  137.2 9.1 %spread.1 = (bf16[6,128,896]{2,1,0:T(8,128)(2,1)S(1)}, bf16[6,128,896]{2,1,0:T(8,128)(2,1)S(1)}, bf16[6,128,896]{2,1,0:T(8,128)(2,1)S(1)}, bf16[6,128,896]{2,1,0:T(8,128)(2,1)}) custom-call(s32[24]{0:T(128)S(1)} %get-tuple-element.94.inv, bf16[2048,512]{1,0:T(8,128)(2,1)} %get-tuple-element.21.dk, bf16[2048,512]{1,0:T(8,128)(2,1)} %get-tuple-element.22.dv, ...), custom_call_target="tpu_custom_call" | custom-call | tf_op jit(solution)/shard_map/spread/pallas_call | solution.py:215
  146.4 3.9 %copy-done.3 = bf16[9984,512]{1,0:T(8,128)(2,1)S(1)} copy-done((bf16[9984,512]{1,0:T(8,128)(2,1)S(1)}, bf16[9984,512]{1,0:T(8,128)(2,1)}, u32[]{:S(2)}) %copy-start.3) | copy-done | bytes 10223640
  150.3 3.9 %unproject.1 = bf16[4,2,128,1024]{3,2,1,0:T(8,128)(2,1)S(1)} custom-call(s32[1]{0:T(128)} %bitcast.n_ref, bf16[128,512]{1,0:T(8,128)(2,1)S(1)} %get-tuple-element.19.ctx, bf16[128,512]{1,0:T(8,128)(2,1)S(1)} %get-tuple-element.20.dq, bf16[32,312,512]{2,1,0:T(8,128)(2,1)S(1)} %bitcast.123), custom_call_target="tpu_custom_call" | custom-call | tf_op jit(solution)/shard_map/unproject/pallas_call | solution.py:236
  154.3 1.4 collective-permute-start.16
  157.4 3.6 %collective-permute-done.16 = bf16[1,128,1024]{2,1,0:T(8,128)(2,1)S(1)} collective-permute-done((bf16[1,128,1024]{2,1,0:T(8,128)(2,1)S(1)}, bf16[1,128,1024]{2,1,0:T(8,128)(2,1)S(1)}, u32[]{:S(2)}, u32[]{:S(2)}) %collective-permute-start.16) | collective-permute-done | bytes 262176 | tf_op jit(solution)/shard_map/ppermute | solution.py:30
  161.0 5.2 %collective-permute-done.12 = bf16[1,128,1024]{2,1,0:T(8,128)(2,1)S(1)} collective-permute-done((bf16[1,128,1024]{2,1,0:T(8,128)(2,1)S(1)}, bf16[1,128,1024]{2,1,0:T(8,128)(2,1)S(1)}, u32[]{:S(2)}, u32[]{:S(2)}) %collective-permute-start.12) | collective-permute-done | bytes 262176 | tf_op jit(solution)/shard_map/ppermute | solution.py:30
  166.8 2.0 collective-permute-start.14
  168.9 2.8 %collective-permute-done.15 = bf16[1,128,1024]{2,1,0:T(8,128)(2,1)S(1)} collective-permute-done((bf16[1,128,1024]{2,1,0:T(8,128)(2,1)S(1)}, bf16[1,128,1024]{2,1,0:T(8,128)(2,1)S(1)}, u32[]{:S(2)}, u32[]{:S(2)}) %collective-permute-start.15) | collective-permute-done | bytes 262176 | tf_op jit(solution)/shard_map/ppermute | solution.py:30
  171.8 3.9 %collective-permute-done.17 = bf16[1,128,1024]{2,1,0:T(8,128)(2,1)S(1)} collective-permute-done((bf16[1,128,1024]{2,1,0:T(8,128)(2,1)S(1)}, bf16[1,128,1024]{2,1,0:T(8,128)(2,1)S(1)}, u32[]{:S(2)}, u32[]{:S(2)}) %collective-permute-start.17) | collective-permute-done | bytes 262176 | tf_op jit(solution)/shard_map/ppermute | solution.py:30
  175.9 10.6 %collective-permute-done.21 = bf16[3,128,896]{2,1,0:T(8,128)(2,1)S(1)} collective-permute-done((bf16[3,128,896]{2,1,0:T(8,128)(2,1)S(1)}, bf16[3,128,896]{2,1,0:T(8,128)(2,1)S(1)}, u32[]{:S(2)}, u32[]{:S(2)}) %collective-permute-start.21) | collective-permute-done | bytes 688160 | tf_op jit(solution)/shard_map/ppermute | solution.py:30
  186.8 3.6 %collective-permute-done.25 = bf16[3,128,896]{2,1,0:T(8,128)(2,1)S(1)} collective-permute-done((bf16[3,128,896]{2,1,0:T(8,128)(2,1)S(1)}, bf16[3,128,896]{2,1,0:T(8,128)(2,1)S(1)}, u32[]{:S(2)}, u32[]{:S(2)}) %collective-permute-start.25) | collective-permute-done | bytes 688160 | tf_op jit(solution)/shard_map/ppermute | solution.py:30
  190.6 1.3 collective-permute-start.26
  191.9 4.2 %collective-permute-done.14 = bf16[1,128,1024]{2,1,0:T(8,128)(2,1)S(1)} collective-permute-done((bf16[1,128,1024]{2,1,0:T(8,128)(2,1)S(1)}, bf16[1,128,1024]{2,1,0:T(8,128)(2,1)S(1)}, u32[]{:S(2)}, u32[]{:S(2)}) %collective-permute-start.14) | collective-permute-done | bytes 262176 | tf_op jit(solution)/shard_map/ppermute | solution.py:30
  196.0 1.2 collective-permute-start.20
  197.2 20.0 %collective-permute-done.20 = f32[128,1]{0,1:T(1,128)S(1)} collective-permute-done((f32[128,1]{0,1:T(1,128)S(1)}, f32[128,1]{0,1:T(1,128)S(1)}, u32[]{:S(2)}, u32[]{:S(2)}) %collective-permute-start.20) | collective-permute-done | bytes 544 | tf_op jit(solution)/shard_map/ppermute | solution.py:30
  217.7 4.7 %collective-permute-done.19 = f32[128,1]{0,1:T(1,128)S(1)} collective-permute-done((f32[128,1]{0,1:T(1,128)S(1)}, f32[128,1]{0,1:T(1,128)S(1)}, u32[]{:S(2)}, u32[]{:S(2)}) %collective-permute-start.19) | collective-permute-done | bytes 544 | tf_op jit(solution)/shard_map/ppermute | solution.py:30
  222.4 4.7 %collective-permute-done.18 = f32[128,1]{0,1:T(1,128)S(1)} collective-permute-done((f32[128,1]{0,1:T(1,128)S(1)}, f32[128,1]{0,1:T(1,128)S(1)}, u32[]{:S(2)}, u32[]{:S(2)}) %collective-permute-start.18) | collective-permute-done | bytes 544 | tf_op jit(solution)/shard_map/ppermute | solution.py:30
  227.2 7.6 %collective-permute-done.13 = bf16[1,128,1024]{2,1,0:T(8,128)(2,1)S(1)} collective-permute-done((bf16[1,128,1024]{2,1,0:T(8,128)(2,1)S(1)}, bf16[1,128,1024]{2,1,0:T(8,128)(2,1)S(1)}, u32[]{:S(2)}, u32[]{:S(2)}) %collective-permute-start.13) | collective-permute-done | bytes 262176 | tf_op jit(solution)/shard_map/ppermute | solution.py:30
  234.7 1.2 subtract_convert_fusion
  236.5 1.2 pad_maximum_fusion.1
  (138 shorter events, 19.2 us)
Async XLA Ops:
  7.2 12.3 %copy-start = (bf16[1024,896]{1,0:T(8,128)(2,1)S(1)}, bf16[1024,896]{1,0:T(8,128)(2,1)}, u32[]{:S(2)}) copy-start(bf16[1024,896]{1,0:T(8,128)(2,1)} %param.18) | copy-start | bytes 5505028
  7.2 7.0 %copy-start.11 = (bf16[128,1024]{1,0:T(8,128)(2,1)S(1)}, bf16[128,1024]{1,0:T(8,128)(2,1)}, u32[]{:S(2)}) copy-start(bf16[128,1024]{1,0:T(8,128)(2,1)} %param.12) | copy-start | bytes 786436
  7.2 11.0 %copy-start.18 = (s32[24]{0:T(128)S(1)}, s32[24]{0:T(128)}, u32[]{:S(2)}) copy-start(s32[24]{0:T(128)} %param.15) | copy-start | bytes 292
  7.2 11.5 %copy-start.12 = (bf16[128,1024]{1,0:T(8,128)(2,1)S(1)}, bf16[128,1024]{1,0:T(8,128)(2,1)}, u32[]{:S(2)}) copy-start(bf16[128,1024]{1,0:T(8,128)(2,1)} %param.13) | copy-start | bytes 786436
  7.2 11.5 %copy-start.16 = (bf16[1024]{0:T(1024)(128)(2,1)S(1)}, bf16[1024]{0:T(1024)(128)(2,1)}, u32[]{:S(2)}) copy-start(bf16[1024]{0:T(1024)(128)(2,1)} %param.16) | copy-start | bytes 6148
  7.2 87.2 %all-gather.3.cloned.1.call-start = ((), (), s32[]{:S(2)}) async-start(), calls=%async_computation.1 | async-start | bytes 10543104 | tf_op jit(solution)/shard_map/all_gather | solution.py:302
  11.0 13.1 %copy-start.17 = (bf16[896]{0:T(1024)(128)(2,1)S(1)}, bf16[896]{0:T(1024)(128)(2,1)}, u32[]{:S(2)}) copy-start(bf16[896]{0:T(1024)(128)(2,1)} %param.17) | copy-start | bytes 5380
  11.0 226.7 %reduce-scatter.4.cloned.1.call-start = ((), (), s32[]{:S(2)}) async-start(), calls=%async_computation.2 | async-start | bytes 6406144
  11.1 57.3 %collective-permute-start.4 = (bf16[6,128,896]{2,1,0:T(8,128)(2,1)}, bf16[6,128,896]{2,1,0:T(8,128)(2,1)}, u32[]{:S(2)}, u32[]{:S(2)}) collective-permute-start(bf16[6,128,896]{2,1,0:T(8,128)(2,1)} %param.14), channel_id=1, source_target_pairs={{0,6},{2,0},{4,2},{6,4},{1,7},{3,1},{5,3},{7,5},{8,14},{10,8},{12,... | collective-permute-start | bytes 4128776 | tf_op jit(solution)/shard_map/ppermute | solution.py:30
  14.2 58.7 %collective-permute-start.6 = (bf16[6,128,896]{2,1,0:T(8,128)(2,1)}, bf16[6,128,896]{2,1,0:T(8,128)(2,1)}, u32[]{:S(2)}, u32[]{:S(2)}) collective-permute-start(bf16[6,128,896]{2,1,0:T(8,128)(2,1)} %param.14), channel_id=1, source_target_pairs={{0,2},{2,4},{4,6},{6,0},{1,3},{3,5},{5,7},{7,1},{8,10},{10,12},{12... | collective-permute-start | bytes 4128776 | tf_op jit(solution)/shard_map/ppermute | solution.py:30
  14.3 5.1 %collective-permute-start = (bf16[1,1024]{1,0:T(2,128)(2,1)S(1)}, bf16[1,1024]{1,0:T(2,128)(2,1)S(1)}, u32[]{:S(2)}, u32[]{:S(2)}) collective-permute-start(bf16[1,1024]{1,0:T(2,128)(2,1)S(1)} %get-tuple-element.80), channel_id=1, source_target_pairs={{0,8},{8,16},{16,24},{24,32},{32,40},{40,48},{48,56},{56,64},{64,7... | collective-permute-start | bytes 6152 | tf_op jit(solution)/shard_map/ppermute | solution.py:308
  18.4 29.7 %copy-start.14 = (bf16[6,128,896]{2,1,0:T(8,128)(2,1)S(1)}, bf16[6,128,896]{2,1,0:T(8,128)(2,1)}, u32[]{:S(2)}) copy-start(bf16[6,128,896]{2,1,0:T(8,128)(2,1)} %param.14) | copy-start | bytes 4128772
  19.5 29.0 %copy-start.20 = (bf16[896,896]{1,0:T(8,128)(2,1)S(1)}, bf16[896,896]{1,0:T(8,128)(2,1)}, u32[]{:S(2)}) copy-start(bf16[896,896]{1,0:T(8,128)(2,1)} %param.19) | copy-start | bytes 4816900
  19.8 24.4 %collective-permute-start.3 = (f32[2,896]{1,0:T(2,128)S(1)}, f32[2,896]{1,0:T(2,128)S(1)}, u32[]{:S(2)}, u32[]{:S(2)}) collective-permute-start(f32[2,896]{1,0:T(2,128)S(1)} %fusion.48), channel_id=1, source_target_pairs={{0,6},{2,0},{4,2},{6,4},{1,7},{3,1},{5,3},{7,5},{8,14},{10,8},{12,... | collective-permute-start | bytes 21512 | tf_op jit(solution)/shard_map/ppermute | solution.py:30
  23.1 23.5 %collective-permute-start.2 = (f32[2,896]{1,0:T(2,128)S(1)}, f32[2,896]{1,0:T(2,128)S(1)}, u32[]{:S(2)}, u32[]{:S(2)}) collective-permute-start(f32[2,896]{1,0:T(2,128)S(1)} %fusion.48), channel_id=1, source_target_pairs={{0,4},{2,6},{4,0},{6,2},{1,5},{3,7},{5,1},{7,3},{8,12},{10,14},{12... | collective-permute-start | bytes 21512 | tf_op jit(solution)/shard_map/ppermute | solution.py:30
  23.1 24.8 %collective-permute-start.1 = (f32[2,896]{1,0:T(2,128)S(1)}, f32[2,896]{1,0:T(2,128)S(1)}, u32[]{:S(2)}, u32[]{:S(2)}) collective-permute-start(f32[2,896]{1,0:T(2,128)S(1)} %fusion.48), channel_id=1, source_target_pairs={{0,2},{2,4},{4,6},{6,0},{1,3},{3,5},{5,7},{7,1},{8,10},{10,12},{12... | collective-permute-start | bytes 21512 | tf_op jit(solution)/shard_map/ppermute | solution.py:30
  44.2 15.2 %collective-permute-start.10 = (bf16[264,1024]{1,0:T(8,128)(2,1)S(1)}, bf16[264,1024]{1,0:T(8,128)(2,1)S(1)}, u32[]{:S(2)}, u32[]{:S(2)}) collective-permute-start(bf16[264,1024]{1,0:T(8,128)(2,1)S(1)} %pad_maximum_fusion.4), channel_id=1, source_target_pairs={{0,2},{2,4},{4,6},{6,0},{1,3},{3,5},{5,7},{7,1},{8,10},{10,12},{12... | collective-permute-start | bytes 1622024 | tf_op jit(solution)/shard_map/ppermute | solution.py:30
  46.6 13.0 %collective-permute-start.8 = (bf16[264,1024]{1,0:T(8,128)(2,1)S(1)}, bf16[264,1024]{1,0:T(8,128)(2,1)S(1)}, u32[]{:S(2)}, u32[]{:S(2)}) collective-permute-start(bf16[264,1024]{1,0:T(8,128)(2,1)S(1)} %pad_maximum_fusion.4), channel_id=1, source_target_pairs={{0,6},{2,0},{4,2},{6,4},{1,7},{3,1},{5,3},{7,5},{8,14},{10,8},{12,... | collective-permute-start | bytes 1622024 | tf_op jit(solution)/shard_map/ppermute | solution.py:30
  59.4 8.0 %collective-permute-start.11 = (bf16[128,1024]{1,0:T(8,128)(2,1)S(1)}, bf16[128,1024]{1,0:T(8,128)(2,1)S(1)}, u32[]{:S(2)}, u32[]{:S(2)}) collective-permute-start(bf16[128,1024]{1,0:T(8,128)(2,1)S(1)} %get-tuple-element.72), channel_id=1, source_target_pairs={{0,2},{2,4},{4,6},{6,0},{1,3},{3,5},{5,7},{7,1},{8,10},{10,12},{12... | collective-permute-start | bytes 786440 | tf_op jit(solution)/shard_map/ppermute | solution.py:30
  59.6 7.9 %collective-permute-start.9 = (bf16[136,1024]{1,0:T(8,128)(2,1)S(1)}, bf16[136,1024]{1,0:T(8,128)(2,1)S(1)}, u32[]{:S(2)}, u32[]{:S(2)}) collective-permute-start(bf16[136,1024]{1,0:T(8,128)(2,1)S(1)} %slice.229), channel_id=1, source_target_pairs={{0,6},{2,0},{4,2},{6,4},{1,7},{3,1},{5,3},{7,5},{8,14},{10,8},{12,... | collective-permute-start | bytes 835592 | tf_op jit(solution)/shard_map/ppermute | solution.py:30
  69.5 18.3 %collective-permute-start.5 = (bf16[3,128,896]{2,1,0:T(8,128)(2,1)S(1)}, bf16[3,128,896]{2,1,0:T(8,128)(2,1)S(1)}, u32[]{:S(2)}, u32[]{:S(2)}) collective-permute-start(bf16[3,128,896]{2,1,0:T(8,128)(2,1)S(1)} %slice.224), channel_id=1, source_target_pairs={{0,6},{2,0},{4,2},{6,4},{1,7},{3,1},{5,3},{7,5},{8,14},{10,8},{12,... | collective-permute-start | bytes 2064392 | tf_op jit(solution)/shard_map/ppermute | solution.py:30
  74.1 15.9 %collective-permute-start.7 = (bf16[3,128,896]{2,1,0:T(8,128)(2,1)S(1)}, bf16[3,128,896]{2,1,0:T(8,128)(2,1)S(1)}, u32[]{:S(2)}, u32[]{:S(2)}) collective-permute-start(bf16[3,128,896]{2,1,0:T(8,128)(2,1)S(1)} %slice.225), channel_id=1, source_target_pairs={{0,2},{2,4},{4,6},{6,0},{1,3},{3,5},{5,7},{7,1},{8,10},{10,12},{12... | collective-permute-start | bytes 2064392 | tf_op jit(solution)/shard_map/ppermute | solution.py:30
  96.0 7.3 %copy-start.4 = (bf16[16,1,56,512]{3,2,1,0:T(8,128)(2,1)}, bf16[16,1,56,512]{3,2,1,0:T(8,128)(2,1)S(1)}, u32[]{:S(2)}) copy-start(bf16[16,1,56,512]{3,2,1,0:T(8,128)(2,1)S(1)} %get-tuple-element.54) | copy-start | bytes 2752516
  96.0 7.3 %copy-start.6 = (bf16[16,1,56,512]{3,2,1,0:T(8,128)(2,1)}, bf16[16,1,56,512]{3,2,1,0:T(8,128)(2,1)S(1)}, u32[]{:S(2)}) copy-start(bf16[16,1,56,512]{3,2,1,0:T(8,128)(2,1)S(1)} %get-tuple-element.55) | copy-start | bytes 2752516
  96.0 4.6 %copy-start.2 = (bf16[9984,512]{1,0:T(8,128)(2,1)S(1)}, bf16[9984,512]{1,0:T(8,128)(2,1)}, u32[]{:S(2)}) copy-start(bf16[9984,512]{1,0:T(8,128)(2,1)} %all-gather.3.cloned.1.call-done) | copy-start | bytes 30670852
  100.6 2.8 %copy-start.8 = (bf16[6,128,896]{2,1,0:T(8,128)(2,1)S(1)}, bf16[6,128,896]{2,1,0:T(8,128)(2,1)}, u32[]{:S(2)}) copy-start(bf16[6,128,896]{2,1,0:T(8,128)(2,1)} %add_convert_fusion.2.e0) | copy-start | bytes 4128772
  100.6 2.8 %copy-start.9 = (bf16[3,128,896]{2,1,0:T(8,128)(2,1)S(1)}, bf16[3,128,896]{2,1,0:T(8,128)(2,1)}, u32[]{:S(2)}) copy-start(bf16[3,128,896]{2,1,0:T(8,128)(2,1)} %add_convert_fusion.8.e2a) | copy-start | bytes 2064388
  100.6 2.8 %copy-start.10 = (bf16[3,128,896]{2,1,0:T(8,128)(2,1)S(1)}, bf16[3,128,896]{2,1,0:T(8,128)(2,1)}, u32[]{:S(2)}) copy-start(bf16[3,128,896]{2,1,0:T(8,128)(2,1)} %add_convert_fusion.7.e2b) | copy-start | bytes 2064388
  121.4 4.9 %copy-start.13 = (bf16[2048,512]{1,0:T(8,128)(2,1)S(1)}, bf16[2048,512]{1,0:T(8,128)(2,1)}, u32[]{:S(2)}) copy-start(bf16[2048,512]{1,0:T(8,128)(2,1)} %get-tuple-element.21.dk) | copy-start | bytes 6291460
  121.4 4.9 %copy-start.19 = (bf16[16,128,896]{2,1,0:T(8,128)(2,1)S(1)}, bf16[16,128,896]{2,1,0:T(8,128)(2,1)}, u32[]{:S(2)}) copy-start(bf16[16,128,896]{2,1,0:T(8,128)(2,1)} %get-tuple-element.27) | copy-start | bytes 11010052
  146.4 3.9 %copy-start.3 = (bf16[9984,512]{1,0:T(8,128)(2,1)S(1)}, bf16[9984,512]{1,0:T(8,128)(2,1)}, u32[]{:S(2)}) copy-start(bf16[9984,512]{1,0:T(8,128)(2,1)} %all-gather.3.cloned.1.call-done) | copy-start | bytes 30670852
  154.3 6.7 %collective-permute-start.16 = (bf16[1,128,1024]{2,1,0:T(8,128)(2,1)S(1)}, bf16[1,128,1024]{2,1,0:T(8,128)(2,1)S(1)}, u32[]{:S(2)}, u32[]{:S(2)}) collective-permute-start(bf16[1,128,1024]{2,1,0:T(8,128)(2,1)S(1)} %get-tuple-element.59), channel_id=1, source_target_pairs={{0,6},{2,0},{4,2},{6,4},{1,7},{3,1},{5,3},{7,5},{8,14},{10,8},{12,... | collective-permute-start | bytes 786440 | tf_op jit(solution)/shard_map/ppermute | solution.py:30
  155.7 10.5 %collective-permute-start.12 = (bf16[1,128,1024]{2,1,0:T(8,128)(2,1)S(1)}, bf16[1,128,1024]{2,1,0:T(8,128)(2,1)S(1)}, u32[]{:S(2)}, u32[]{:S(2)}) collective-permute-start(bf16[1,128,1024]{2,1,0:T(8,128)(2,1)S(1)} %get-tuple-element.61), channel_id=1, source_target_pairs={{0,2},{2,4},{4,6},{6,0},{1,3},{3,5},{5,7},{7,1},{8,10},{10,12},{12... | collective-permute-start | bytes 786440 | tf_op jit(solution)/shard_map/ppermute | solution.py:30
  156.7 15.1 %collective-permute-start.15 = (bf16[1,128,1024]{2,1,0:T(8,128)(2,1)S(1)}, bf16[1,128,1024]{2,1,0:T(8,128)(2,1)S(1)}, u32[]{:S(2)}, u32[]{:S(2)}) collective-permute-start(bf16[1,128,1024]{2,1,0:T(8,128)(2,1)S(1)} %get-tuple-element.58), channel_id=1, source_target_pairs={{0,2},{2,4},{4,6},{6,0},{1,3},{3,5},{5,7},{7,1},{8,10},{10,12},{12... | collective-permute-start | bytes 786440 | tf_op jit(solution)/shard_map/ppermute | solution.py:30
  156.7 12.1 %copy-start.15 = (bf16[6,128,896]{2,1,0:T(8,128)(2,1)S(1)}, bf16[6,128,896]{2,1,0:T(8,128)(2,1)}, u32[]{:S(2)}) copy-start(bf16[6,128,896]{2,1,0:T(8,128)(2,1)} %get-tuple-element.26) | copy-start | bytes 4128772
  156.8 29.7 %collective-permute-start.21 = (bf16[3,128,896]{2,1,0:T(8,128)(2,1)S(1)}, bf16[3,128,896]{2,1,0:T(8,128)(2,1)S(1)}, u32[]{:S(2)}, u32[]{:S(2)}) collective-permute-start(bf16[3,128,896]{2,1,0:T(8,128)(2,1)S(1)} %get-tuple-element.66), channel_id=1, source_target_pairs={{0,2},{2,4},{4,6},{6,0},{1,3},{3,5},{5,7},{7,1},{8,10},{10,12},{12... | collective-permute-start | bytes 2064392 | tf_op jit(solution)/shard_map/ppermute | solution.py:30
  166.4 9.3 %collective-permute-start.17 = (bf16[1,128,1024]{2,1,0:T(8,128)(2,1)S(1)}, bf16[1,128,1024]{2,1,0:T(8,128)(2,1)S(1)}, u32[]{:S(2)}, u32[]{:S(2)}) collective-permute-start(bf16[1,128,1024]{2,1,0:T(8,128)(2,1)S(1)} %get-tuple-element.62), channel_id=1, source_target_pairs={{0,6},{2,0},{4,2},{6,4},{1,7},{3,1},{5,3},{7,5},{8,14},{10,8},{12,... | collective-permute-start | bytes 786440 | tf_op jit(solution)/shard_map/ppermute | solution.py:30
  166.4 24.0 %collective-permute-start.25 = (bf16[3,128,896]{2,1,0:T(8,128)(2,1)S(1)}, bf16[3,128,896]{2,1,0:T(8,128)(2,1)S(1)}, u32[]{:S(2)}, u32[]{:S(2)}) collective-permute-start(bf16[3,128,896]{2,1,0:T(8,128)(2,1)S(1)} %get-tuple-element.67), channel_id=1, source_target_pairs={{0,6},{2,0},{4,2},{6,4},{1,7},{3,1},{5,3},{7,5},{8,14},{10,8},{12,... | collective-permute-start | bytes 2064392 | tf_op jit(solution)/shard_map/ppermute | solution.py:30
  166.8 29.3 %collective-permute-start.14 = (bf16[1,128,1024]{2,1,0:T(8,128)(2,1)S(1)}, bf16[1,128,1024]{2,1,0:T(8,128)(2,1)S(1)}, u32[]{:S(2)}, u32[]{:S(2)}) collective-permute-start(bf16[1,128,1024]{2,1,0:T(8,128)(2,1)S(1)} %get-tuple-element.60), channel_id=1, source_target_pairs={{0,6},{2,0},{4,2},{6,4},{1,7},{3,1},{5,3},{7,5},{8,14},{10,8},{12,... | collective-permute-start | bytes 786440 | tf_op jit(solution)/shard_map/ppermute | solution.py:30
  171.8 64.1 %collective-permute-start.23 = (bf16[3,128,896]{2,1,0:T(8,128)(2,1)S(1)}, bf16[3,128,896]{2,1,0:T(8,128)(2,1)S(1)}, u32[]{:S(2)}, u32[]{:S(2)}) collective-permute-start(bf16[3,128,896]{2,1,0:T(8,128)(2,1)S(1)} %slice.209), channel_id=1, source_target_pairs={{0,6},{2,0},{4,2},{6,4},{1,7},{3,1},{5,3},{7,5},{8,14},{10,8},{12,... | collective-permute-start | bytes 2064392 | tf_op jit(solution)/shard_map/ppermute | solution.py:30
  175.7 60.2 %collective-permute-start.24 = (bf16[3,128,896]{2,1,0:T(8,128)(2,1)S(1)}, bf16[3,128,896]{2,1,0:T(8,128)(2,1)S(1)}, u32[]{:S(2)}, u32[]{:S(2)}) collective-permute-start(bf16[3,128,896]{2,1,0:T(8,128)(2,1)S(1)} %slice.211), channel_id=1, source_target_pairs={{0,2},{2,4},{4,6},{6,0},{1,3},{3,5},{5,7},{7,1},{8,10},{10,12},{12... | collective-permute-start | bytes 2064392 | tf_op jit(solution)/shard_map/ppermute | solution.py:30
  186.7 49.2 %collective-permute-start.22 = (bf16[3,128,896]{2,1,0:T(8,128)(2,1)S(1)}, bf16[3,128,896]{2,1,0:T(8,128)(2,1)S(1)}, u32[]{:S(2)}, u32[]{:S(2)}) collective-permute-start(bf16[3,128,896]{2,1,0:T(8,128)(2,1)S(1)} %add_convert_fusion.6), channel_id=1, source_target_pairs={{0,2},{2,4},{4,6},{6,0},{1,3},{3,5},{5,7},{7,1},{8,10},{10,12},{12... | collective-permute-start | bytes 2064392 | tf_op jit(solution)/shard_map/ppermute | solution.py:30
  190.6 45.3 %collective-permute-start.26 = (bf16[3,128,896]{2,1,0:T(8,128)(2,1)S(1)}, bf16[3,128,896]{2,1,0:T(8,128)(2,1)S(1)}, u32[]{:S(2)}, u32[]{:S(2)}) collective-permute-start(bf16[3,128,896]{2,1,0:T(8,128)(2,1)S(1)} %add_convert_fusion.4), channel_id=1, source_target_pairs={{0,6},{2,0},{4,2},{6,4},{1,7},{3,1},{5,3},{7,5},{8,14},{10,8},{12,... | collective-permute-start | bytes 2064392 | tf_op jit(solution)/shard_map/ppermute | solution.py:30
  196.0 21.3 %collective-permute-start.20 = (f32[128,1]{0,1:T(1,128)S(1)}, f32[128,1]{0,1:T(1,128)S(1)}, u32[]{:S(2)}, u32[]{:S(2)}) collective-permute-start(f32[128,1]{0,1:T(1,128)S(1)} %multiply_bitcast_fusion), channel_id=1, source_target_pairs={{0,6},{2,0},{4,2},{6,4},{1,7},{3,1},{5,3},{7,5},{8,14},{10,8},{12,... | collective-permute-start | bytes 1544 | tf_op jit(solution)/shard_map/ppermute | solution.py:30
  217.3 5.1 %collective-permute-start.19 = (f32[128,1]{0,1:T(1,128)S(1)}, f32[128,1]{0,1:T(1,128)S(1)}, u32[]{:S(2)}, u32[]{:S(2)}) collective-permute-start(f32[128,1]{0,1:T(1,128)S(1)} %multiply_bitcast_fusion), channel_id=1, source_target_pairs={{0,4},{2,6},{4,0},{6,2},{1,5},{3,7},{5,1},{7,3},{8,12},{10,14},{12... | collective-permute-start | bytes 1544 | tf_op jit(solution)/shard_map/ppermute | solution.py:30
  222.4 4.8 %collective-permute-start.18 = (f32[128,1]{0,1:T(1,128)S(1)}, f32[128,1]{0,1:T(1,128)S(1)}, u32[]{:S(2)}, u32[]{:S(2)}) collective-permute-start(f32[128,1]{0,1:T(1,128)S(1)} %multiply_bitcast_fusion), channel_id=1, source_target_pairs={{0,2},{2,4},{4,6},{6,0},{1,3},{3,5},{5,7},{7,1},{8,10},{10,12},{12... | collective-permute-start | bytes 1544 | tf_op jit(solution)/shard_map/ppermute | solution.py:30
  227.2 7.6 %collective-permute-start.13 = (bf16[1,128,1024]{2,1,0:T(8,128)(2,1)S(1)}, bf16[1,128,1024]{2,1,0:T(8,128)(2,1)S(1)}, u32[]{:S(2)}, u32[]{:S(2)}) collective-permute-start(bf16[1,128,1024]{2,1,0:T(8,128)(2,1)S(1)} %get-tuple-element.63), channel_id=1, source_target_pairs={{0,2},{2,4},{4,6},{6,0},{1,3},{3,5},{5,7},{7,1},{8,10},{10,12},{12... | collective-permute-start | bytes 786440 | tf_op jit(solution)/shard_map/ppermute | solution.py:30
  236.5 4.0 %copy-start.1 = (bf16[1024,896]{1,0:T(8,128)(2,1)S(1)}, bf16[1024,896]{1,0:T(8,128)(2,1)}, u32[]{:S(2)}) copy-start(bf16[1024,896]{1,0:T(8,128)(2,1)} %param.18) | copy-start | bytes 5505028
  (2 other events, 2.4 us)
Sparse Core Ops, SparseCore 0:
  11.1 59.7 all-gather.2
  135.0 80.9 reduce-scatter.3
